TPU v7x, 32 devices: a whole 2x2x4 slice. The times are simulated.
32 devices in a mesh: groups: 2 (over y), space: 4 (over z), tm: 2 (over x), comp: 2 (over core).
Axes of the slice: x: 2, y: 2, z: 4, core: 2. Of those that a mesh axis runs over, the one named last changes fastest.
Arguments:
- stored: float32 [4096, 4, 3, 512], P(('groups', 'space', 'comp'), 'tm'), parts along dimension 0, may hold values from -6 to 6
- brick_ids: int32 [4096], P(('groups', 'space', 'comp')), parts along dimension 0, may hold values from 0 to 1073741823, as said below
- brick_counts: int32 [16], P(('groups', 'space', 'comp')), parts along dimension 0, may hold values from 0 to 256
- snapshot_ids: int32 [8], P('groups'), parts along dimension 0, may hold values from 999 to 1008, as said below
- between: float32 [2], P('groups'), parts along dimension 0, may hold values from 0.05 to 0.95
- anchor: int32 [6], P('groups'), parts along dimension 0, may hold values from 0 to 1016, as said below
Outputs:
- vorticity: float32 [3, 128, 64, 128], P(None, ('groups', 'space', 'tm'), 'comp'), parts along dimension 1
There are 2 independent parts, one for each index of `groups`. A program takes and returns all parts, laid end to end along the dimension named above; each array names one. Nothing has to cross between parts.
Inputs may be any that keep to these rules, and one draw needn't show every extreme that they name: `brick_ids`: the live slots of each device hold distinct codes, ascending; all live slots together name every brick of the cutout once. Slots past a device's count hold meaningless codes. With a tile being the cells x in [s * 16, (s + 1) * 16) and y in [c * 32, (c + 1) * 32) for device index s * 2 + c over space+comp: one device holds at most 32 bricks of one tile, and the devices of one space index hold exactly 32 bricks of each tile together. `snapshot_ids`: strictly increasing, by 1 to 3 from one to the next; the last is 1008. `anchor`: each entry plus the cutout's extent in bricks along that dimension is at most 1024.
All inputs are finite; a program needn't handle non-finite values.
Results may differ from a plain program's by a relative error of at most 0.00002.
Values sent between devices are 32-bit elements; how exact they have to be, the bound alone decides.
No kernel may reach another device: no remote copies, remote signals or barrier semaphores. Data moves between devices by JAX's collectives and lax.ppermute only.
A program may use at most 128 MiB of HBM per device.

v0:
```python
import jax
import jax.numpy as jnp
from jax import lax
from jax.sharding import PartitionSpec as P

BRICK = 8
GRID = 1024
CXD = 8
CY = 32
NZ = 128


coefficients = (0.8, -0.2, 4.0 / 105.0, -1.0 / 280.0)


def extended(shard, sides, width):
    for axis, dim in sides:
        size, length = (lax.axis_size(axis), shard.shape[dim])
        up = [(i, (i + 1) % size) for i in range(size)]
        down = [(j, i) for i, j in up]
        last = lax.slice_in_dim(shard, length - width, length, axis=dim)
        initial = lax.slice_in_dim(shard, 0, width, axis=dim)
        before = lax.ppermute(last, axis, up)
        after = lax.ppermute(initial, axis, down)
        shard = jnp.concatenate([before, shard, after], axis=dim)
    return shard


def hermite_weights(snapshot_ids, between):
    stamps = snapshot_ids.astype(jnp.float32)
    fraction = between[0]
    square = fraction * fraction
    cubed = square * fraction
    spacing = stamps[2] - stamps[1]
    first_base = 2.0 * cubed - 3.0 * square + 1.0
    first_slope = cubed - 2.0 * square + fraction
    second_base = 3.0 * square - 2.0 * cubed
    second_slope = cubed - square
    left_gain = first_slope * spacing / (stamps[2] - stamps[0])
    right_gain = second_slope * spacing / (stamps[3] - stamps[1])
    return jnp.stack([-left_gain, first_base - right_gain, second_base + left_gain, right_gain])


def decode_morton(morton):
    levels = GRID.bit_length() - 1
    decoded = []
    for offset in (2, 1, 0):
        coordinate = jnp.zeros_like(morton)
        for level in range(levels):
            coordinate = coordinate | (jnp.right_shift(morton, 3 * level + offset) & 1) << level
        decoded.append(coordinate)
    return decoded


def rank_within(labels, live_flags, buckets):
    onehot = (
        (labels[:, None] == jnp.arange(buckets, dtype=jnp.int32)[None, :]) & live_flags[:, None]
    ).astype(jnp.int32)
    before = jnp.cumsum(onehot, axis=0) - onehot
    return jnp.sum(before * onehot, axis=1)


def pack_rows(rows, places, slot_of, total):
    packed = jnp.zeros((total + 1,) + rows.shape[1:], rows.dtype).at[slot_of].set(rows)[:total]
    packed_places = jnp.full((total + 1,), -1.0, jnp.float32).at[slot_of].set(places)[:total]
    return (packed, packed_places)


def centred(padded, axis_number, reach):
    extent = padded.shape[axis_number] - 2 * reach
    total = 0.0
    for distance, coefficient in enumerate(coefficients, start=1):
        ahead = lax.slice_in_dim(
            padded, reach + distance, reach + distance + extent, axis=axis_number
        )
        behind = lax.slice_in_dim(
            padded, reach - distance, reach - distance + extent, axis=axis_number
        )
        total = total + coefficient * (ahead - behind)
    return total


def periodic(field, axis_number):
    total = 0.0
    for distance, coefficient in enumerate(coefficients, start=1):
        total = total + coefficient * (
            jnp.roll(field, -distance, axis_number) - jnp.roll(field, distance, axis_number)
        )
    return total


def body(stored, brick_ids, brick_counts, snapshot_ids, between, anchor):
    space_count = lax.axis_size("space")
    time_count = lax.axis_size("tm")
    comp_count = lax.axis_size("comp")
    device_count = space_count * comp_count
    bricks_across = CXD * time_count // BRICK
    bricks_along = CY // BRICK
    bricks_deep = NZ // BRICK
    tile_bricks = bricks_across * bricks_along * bricks_deep
    capacity = tile_bricks // space_count
    weights = hermite_weights(snapshot_ids, between)
    local_snaps = stored.shape[1]
    mine = lax.dynamic_slice_in_dim(weights, lax.axis_index("tm") * local_snaps, local_snaps)
    all_live = jnp.arange(stored.shape[0], dtype=jnp.int32) < brick_counts[0]
    weighted = mine[0] * stored[:, 0]
    for snapshot in range(1, local_snaps):
        weighted = weighted + mine[snapshot] * stored[:, snapshot]
    share = stored.shape[0] // time_count
    source_rows = lax.psum_scatter(weighted, "tm", scatter_dimension=0, tiled=True)
    first_slot = lax.axis_index("tm") * share
    source_ids = lax.dynamic_slice_in_dim(brick_ids, first_slot, share)
    live_flags = lax.dynamic_slice_in_dim(all_live, first_slot, share)
    row_shape = source_rows.shape[1:]
    across, along, depth = decode_morton(source_ids)
    local_x = jnp.mod(across - anchor[0], space_count * bricks_across)
    local_y = jnp.mod(along - anchor[1], comp_count * bricks_along)
    local_z = jnp.mod(depth - anchor[2], bricks_deep)
    target = local_x // bricks_across * comp_count + local_y // bricks_along
    places = (
        local_x % bricks_across * bricks_along + local_y % bricks_along
    ) * bricks_deep + local_z
    places = places.astype(jnp.float32)
    ranks = rank_within(target, live_flags, device_count)
    total = device_count * capacity
    slot_of = jnp.where(live_flags, target * capacity + ranks, total)
    rows, row_places = pack_rows(source_rows, places, slot_of, total)
    rows = rows.reshape((device_count, capacity) + row_shape)
    row_places = row_places.reshape(device_count, capacity)
    rows, row_places = (
        lax.all_to_all(rows, ("space", "comp"), split_axis=0, concat_axis=0, tiled=True),
        lax.all_to_all(row_places, ("space", "comp"), split_axis=0, concat_axis=0, tiled=True),
    )
    rows = rows.reshape((total,) + row_shape)
    row_places = row_places.reshape(total)
    landing = jnp.where(row_places >= 0.0, row_places, float(tile_bricks)).astype(jnp.int32)
    tile = (
        jnp.zeros((tile_bricks + 1,) + row_shape, jnp.float32).at[landing].set(rows)[:tile_bricks]
    )
    slab = tile.reshape(bricks_across, bricks_along, bricks_deep, 3, BRICK, BRICK, BRICK)
    slab = slab.transpose(3, 0, 4, 1, 5, 2, 6).reshape(3, bricks_across * BRICK, CY, NZ)
    velocity = lax.psum_scatter(slab, "tm", scatter_dimension=1, tiled=True)
    reach = len(coefficients)
    padded = extended(velocity, ((("space", "tm"), 1), ("comp", 2)), reach)
    inner_rows = lax.slice_in_dim(padded, reach, padded.shape[1] - reach, axis=1)
    inner_cols = lax.slice_in_dim(padded, reach, padded.shape[2] - reach, axis=2)
    interior = lax.slice_in_dim(inner_rows, reach, inner_rows.shape[2] - reach, axis=2)
    d_dx = centred(inner_cols[1:3], 1, reach)
    d_dy = centred(inner_rows[0::2], 2, reach)
    d_dz = periodic(interior[0:2], 3)
    return jnp.stack([d_dy[1] - d_dz[1], d_dz[0] - d_dx[1], d_dx[0] - d_dy[0]])


def solution(mesh):
    return jax.shard_map(
        body,
        mesh=mesh,
        in_specs=(
            P(("groups", "space", "comp"), "tm", None, None),
            P(("groups", "space", "comp")),
            P(("groups", "space", "comp")),
            P("groups"),
            P("groups"),
            P("groups"),
        ),
        out_specs=P(None, ("groups", "space", "tm"), "comp", None),
        check_vma=False,
    )
```

profile of v0, /device:TPU:11, one launch (start us, length us, event | category | flops | bytes accessed | tf_op | source)
XLA Modules:
  0.0 175.5 jit_solution(13447968887774486038)
XLA Ops:
  7.2 0.7 convert_element_type.22
  7.9 0.7 fusion.47
  12.6 0.7 fusion.46
  13.2 5.5 %fusion.35 = (f32[256,1,3,512]{3,1,2,0:T(1,128)S(1)}, f32[256,1,3,512]{3,1,2,0:T(1,128)S(1)}) fusion(f32[256,2,3,512]{3,1,2,0:T(2,128)} %param.6), kind=kLoop, calls=%fused_computation.93 | loop fusion | bytes 6291456 | tf_op jit(solution)/shard_map/slice | solution.py:106
  18.8 2.9 %fusion.1 = f32[256,3,512]{2,0,1:T(8,128)} fusion(f32[256,1,3,512]{3,1,2,0:T(1,128)S(1)} %get-tuple-element.9, f32[256,1,3,512]{3,1,2,0:T(1,128)S(1)} %get-tuple-element.8, f32[]{:T(128)} %bitcast.18, f32[]{:T(128)} %bitcast.17), kind=kLoop, calls=%fused_computation.5 | loop fusion | flops 1179648 | bytes 4718600 | tf_op jit(solution)/shard_map/add | solution.py:108
  22.4 0.6 fusion.48
  23.1 1.9 %fusion.34 = (f32[128]{0:T(128)S(1)}, s32[128]{0:T(128)S(1)}, s32[128]{0:T(128)S(1)}) fusion(s32[]{:T(128)} %bitcast.7, s32[256]{0:T(256)S(1)} %copy-done.2, s32[]{:T(128)S(6)} %select_n.67, s32[]{:T(128)} %bitcast.6, s32[]{:T(128)} %bitcast.5), kind=kLoop, calls=%fused_computation.92 | loop fusion | flops 23040 | bytes 2064 | tf_op jit(solution)/shard_map/convert_element_type | solution.py:123
  25.2 0.2 reduce_window_sum.11
  25.3 0.2 select_reduce_fusion
  25.6 1.0 scatter_custom_fusion
  26.6 0.7 all_to_all.9
  27.3 5.6 %all-to-all-start = ((f32[8,1,32]{2,1,0:T(1,128)}), f32[8,1,32]{2,1,0:T(1,128)S(1)}, u32[]{:S(2)}, u32[]{:S(2)}) async-start(f32[8,1,32]{2,1,0:T(1,128)} %all_to_all.9), calls=%async_computation | async-start | bytes 8192 | tf_op jit(solution)/shard_map/all_to_all | solution.py:132
  32.9 15.2 %reduce-scatter.6.cloned.1.call-done = f32[128,3,512]{2,0,1:T(8,128)} async-done(((f32[256,3,512]{2,0,1:T(8,128)}), f32[128,3,512]{2,0,1:T(8,128)}) %reduce-scatter.6.cloned.1.call-update) | async-done | bytes 786448 | tf_op jit(solution)/shard_map/reduce_scatter | solution.py:110
  48.1 1.7 copy.19
  49.7 0.3 broadcast_in_dim.30
  50.0 4.7 %scatter_fusion = f32[257,3,512]{2,1,0:T(4,128)S(1)} fusion(f32[257,3,512]{2,1,0:T(4,128)S(1)} %broadcast_in_dim.30, s32[128]{0:T(128)S(1)} %compare_select_fusion.2, f32[128,3,512]{2,1,0:T(4,128)S(1)} %copy.19), kind=kCustom, calls=%fused_computation.1 | custom fusion | bytes 2359808 | tf_op jit(solution)/shard_map/scatter | solution.py:64
  54.7 0.4 slice.292
  55.1 1.7 copy.21
  56.8 5.6 %all-to-all-start.1 = ((f32[8,32,3,512]{3,1,2,0:T(8,128)}), f32[8,32,3,512]{3,1,2,0:T(8,128)S(1)}, u32[]{:S(2)}, u32[]{:S(2)}) async-start(f32[8,32,3,512]{3,1,2,0:T(8,128)} %copy.21), calls=%async_computation.2 | async-start | bytes 3145728 | tf_op jit(solution)/shard_map/all_to_all | solution.py:131
  62.4 0.5 broadcast.215
  62.9 0.7 reduce.3
  63.6 33.0 %all-to-all-done.1 = f32[8,32,3,512]{3,1,2,0:T(8,128)S(1)} async-done(((f32[8,32,3,512]{3,1,2,0:T(8,128)}), f32[8,32,3,512]{3,1,2,0:T(8,128)S(1)}, u32[]{:S(2)}, u32[]{:S(2)}) %all-to-all-start.1) | async-done | bytes 1572896 | tf_op jit(solution)/shard_map/all_to_all | solution.py:131
  96.8 1.1 copy.23
  97.9 0.1 broadcast_in_dim.25
  98.0 7.6 %scatter_fusion.1 = f32[129,3,512]{2,1,0:T(4,128)S(1)} fusion(f32[129,3,512]{2,1,0:T(4,128)S(1)} %broadcast_in_dim.25, s32[256]{0:T(256)S(1)} %bitcast.65, f32[256,3,512]{2,1,0:T(4,128)S(1)} %copy.23), kind=kCustom, calls=%fused_computation.2 | custom fusion | bytes 4719616 | tf_op jit(solution)/shard_map/scatter | solution.py:138
  105.6 0.2 slice.293
  105.8 0.3 copy.24
  106.1 5.6 %reshape.64 = f32[2,4,16,3,8,8,8]{2,1,0,6,5,4,3:T(4,128)} reshape(f32[128,3,512]{0,2,1:T(8,128)S(1)} %copy.24) | data formatting | bytes 1572864 | tf_op jit(solution)/shard_map/reshape | solution.py:140
  111.7 10.4 %copy.30 = f32[3,2,8,4,8,16,8]{6,5,4,3,0,2,1:T(8,128)} copy(f32[3,2,8,4,8,16,8]{5,3,1,6,4,2,0:T(4,128)} %bitcast.59) | data formatting | bytes 1572864
  122.1 9.1 %reshape.94 = f32[3,16,32,128]{3,2,0,1:T(8,128)S(1)} reshape(f32[3,2,8,4,8,16,8]{6,5,4,3,0,2,1:T(8,128)} %copy.30) | data formatting | bytes 1572864
  131.2 1.4 copy.67
  132.6 18.1 %reduce-scatter.8.cloned.1.call-done = f32[8,12288]{1,0:T(8,128)} async-done(((f32[16,12288]{1,0:T(8,128)}), f32[8,12288]{1,0:T(8,128)}) %reduce-scatter.8.cloned.1.call-update) | async-done | bytes 393232
  150.7 1.2 fusion.45
  152.0 1.2 fusion.39
  153.3 0.1 fusion.43
  153.4 0.1 fusion.44
  153.6 0.1 fusion.41
  153.7 0.1 fusion.38
  154.1 2.2 %collective-permute-start = (f32[3,4,32,128]{3,2,1,0:T(8,128)S(1)}, f32[3,4,32,128]{3,2,1,0:T(8,128)S(1)}, u32[]{:S(2)}, u32[]{:S(2)}) collective-permute-start(f32[3,4,32,128]{3,2,1,0:T(8,128)S(1)} %copy.49), channel_id=1, source_target_pairs={{0,2},{2,4},{4,6},{6,8},{8,10},{10,12},{12,14},{14,0},{1,3},{3,5},... | collective-permute-start | bytes 589832 | tf_op jit(solution)/shard_map/ppermute | solution.py:23
  157.4 2.4 %collective-permute-done = f32[3,4,32,128]{3,2,1,0:T(8,128)S(1)} collective-permute-done((f32[3,4,32,128]{3,2,1,0:T(8,128)S(1)}, f32[3,4,32,128]{3,2,1,0:T(8,128)S(1)}, u32[]{:S(2)}, u32[]{:S(2)}) %collective-permute-start) | collective-permute-done | bytes 196640 | tf_op jit(solution)/shard_map/ppermute | solution.py:23
  159.8 0.1 constant_dynamic-update-slice_fusion.4
  160.0 5.1 %collective-permute-done.1 = f32[3,4,32,128]{3,2,1,0:T(8,128)S(1)} collective-permute-done((f32[3,4,32,128]{3,2,1,0:T(8,128)S(1)}, f32[3,4,32,128]{3,2,1,0:T(8,128)S(1)}, u32[]{:S(2)}, u32[]{:S(2)}) %collective-permute-start.1) | collective-permute-done | bytes 196640 | tf_op jit(solution)/shard_map/ppermute | solution.py:24
  165.2 0.9 collective-permute-start.2
  166.2 0.6 fusion.19
  166.8 0.2 collective-permute-done.2
  167.0 0.4 collective-permute-done.3
  167.5 0.3 fusion.3
  167.8 0.8 pad_maximum_fusion.2
  (52 shorter events, 2.4 us)
Async XLA Ops:
  6.5 41.5 %reduce-scatter.6.cloned.1.call-start = ((), (), s32[]{:S(2)}) async-start(), calls=%async_computation.4 | async-start | bytes 2359296 | tf_op jit(solution)/shard_map/reduce_scatter | solution.py:110
  21.7 0.8 copy-start.1
  21.7 1.4 copy-start.2
  27.3 29.5 %all-to-all-start = ((f32[8,1,32]{2,1,0:T(1,128)}), f32[8,1,32]{2,1,0:T(1,128)S(1)}, u32[]{:S(2)}, u32[]{:S(2)}) async-start(f32[8,1,32]{2,1,0:T(1,128)} %all_to_all.9), calls=%async_computation | async-start | bytes 8192 | tf_op jit(solution)/shard_map/all_to_all | solution.py:132
  56.8 39.9 %all-to-all-start.1 = ((f32[8,32,3,512]{3,1,2,0:T(8,128)}), f32[8,32,3,512]{3,1,2,0:T(8,128)S(1)}, u32[]{:S(2)}, u32[]{:S(2)}) async-start(f32[8,32,3,512]{3,1,2,0:T(8,128)} %copy.21), calls=%async_computation.2 | async-start | bytes 3145728 | tf_op jit(solution)/shard_map/all_to_all | solution.py:131
  62.4 88.4 %reduce-scatter.8.cloned.1.call-start = ((), (), s32[]{:S(2)}) async-start(), calls=%async_computation.5 | async-start | bytes 1179648
  150.7 2.4 %copy-start = (f32[8,12288]{1,0:T(8,128)S(1)}, f32[8,12288]{1,0:T(8,128)}, u32[]{:S(2)}) copy-start(f32[8,12288]{1,0:T(8,128)} %reduce-scatter.8.cloned.1.call-done) | copy-start | bytes 1179652
  154.1 5.7 %collective-permute-start = (f32[3,4,32,128]{3,2,1,0:T(8,128)S(1)}, f32[3,4,32,128]{3,2,1,0:T(8,128)S(1)}, u32[]{:S(2)}, u32[]{:S(2)}) collective-permute-start(f32[3,4,32,128]{3,2,1,0:T(8,128)S(1)} %copy.49), channel_id=1, source_target_pairs={{0,2},{2,4},{4,6},{6,8},{8,10},{10,12},{12,14},{14,0},{1,3},{3,5},... | collective-permute-start | bytes 589832 | tf_op jit(solution)/shard_map/ppermute | solution.py:23
  156.3 8.8 %collective-permute-start.1 = (f32[3,4,32,128]{3,2,1,0:T(8,128)S(1)}, f32[3,4,32,128]{3,2,1,0:T(8,128)S(1)}, u32[]{:S(2)}, u32[]{:S(2)}) collective-permute-start(f32[3,4,32,128]{3,2,1,0:T(8,128)S(1)} %copy.50), channel_id=1, source_target_pairs={{2,0},{4,2},{6,4},{8,6},{10,8},{12,10},{14,12},{0,14},{3,1},{5,3},... | collective-permute-start | bytes 589832 | tf_op jit(solution)/shard_map/ppermute | solution.py:24
  165.2 1.8 %collective-permute-start.2 = (f32[3,16,4,128]{3,2,1,0:T(4,128)S(1)}, f32[3,16,4,128]{3,2,1,0:T(4,128)S(1)}, u32[]{:S(2)}, u32[]{:S(2)}) collective-permute-start(f32[3,16,4,128]{3,2,1,0:T(4,128)S(1)} %get-tuple-element.10), channel_id=1, source_target_pairs={{0,1},{1,0},{2,3},{3,2},{4,5},{5,4},{6,7},{7,6},{8,9},{9,8},{10,11... | collective-permute-start | bytes 294920 | tf_op jit(solution)/shard_map/ppermute | solution.py:23
  166.1 1.3 collective-permute-start.3
Sparse Core Ops, SparseCore 0:
  21.8 26.1 reduce-scatter.5
  132.7 17.9 reduce-scatter.7
where the time goes:
time: 179 us; the launch traced here: 175 us
  waiting for transfers between devices  74.5 us (42%)
  local copies, waits for them, and re-layouts  59 us (33%)
  between operations  19 us (11%)
  starting transfers between devices  14.3 us (8%)
  other arithmetic  8.58 us (5%)
    all_to_all x1, waiting for transfers between devices, body(): lax.all_to_all(rows, ('space', 'comp'), split_axis=0, concat_axis=0, tile...  33 us
    unnamed x30, local copies, waits for them, and re-layouts  21.9 us
    unnamed x3, waiting for transfers between devices  18.2 us
    reduce_scatter x1, waiting for transfers between devices, body(): lax.psum_scatter(weighted, 'tm', scatter_dimension=0, tiled=True)  15.2 us
    scatter x1, local copies, waits for them, and re-layouts, body(): jnp.zeros((tile_bricks + 1,) + row_shape, jnp.float32).at[landing].set(rows)  7.56 us
    slice x2, local copies, waits for them, and re-layouts, body(): weighted = mine[0] * stored[:, 0]  6.2 us
    all_to_all x1, starting transfers between devices, body(): lax.all_to_all(rows, ('space', 'comp'), split_axis=0, concat_axis=0, tile...  5.61 us
    all_to_all x1, starting transfers between devices, body(): lax.all_to_all(row_places, ('space', 'comp'), split_axis=0, concat_axis=0...  5.6 us
  transfers between devices with their start and end apart: 8, of which 7 were waited for; matrix products, arithmetic and copies ran while one was open for 9% of the time, Pallas kernels for 0%

commit v1 on v0

v1 whole, which is shorter than its diff:
```python
import functools

import jax
import jax.numpy as jnp
from jax import lax
from jax.experimental import pallas as pl
from jax.experimental.pallas import tpu as pltpu
from jax.sharding import PartitionSpec as P

BRICK = 8
GRID = 1024
CXD = 8
CY = 32
NZ = 128
LANES = 128
ROWS = BRICK**3 // LANES
REACH = 4

coefficients = (0.8, -0.2, 4.0 / 105.0, -1.0 / 280.0)

VMEM = pl.BlockSpec(memory_space=pltpu.VMEM)
SMEM = pl.BlockSpec(memory_space=pltpu.SMEM)
HBM = pl.BlockSpec(memory_space=pl.ANY)
f32 = jnp.float32
bf16 = jnp.bfloat16


def thirds(value):
    high = value.astype(bf16)
    rest = value - high.astype(f32)
    middle = rest.astype(bf16)
    low = (rest - middle.astype(f32)).astype(bf16)
    return high, middle, low


def select_rows(onehot, value):
    total = None
    for part in thirds(value):
        product = jnp.dot(onehot, part, preferred_element_type=f32)
        total = product if total is None else total + product
    return total


def hermite_weights(snapshot_ref, between_ref, first, count):
    shape = (8, LANES)
    stamps = [jnp.full(shape, snapshot_ref[i], jnp.int32).astype(f32) for i in range(4)]
    fraction = jnp.full(shape, between_ref[0], f32)
    square = fraction * fraction
    cubed = square * fraction
    spacing = stamps[2] - stamps[1]
    first_base = 2.0 * cubed - 3.0 * square + 1.0
    first_slope = cubed - 2.0 * square + fraction
    second_base = 3.0 * square - 2.0 * cubed
    second_slope = cubed - square
    left_gain = first_slope * spacing / (stamps[2] - stamps[0])
    right_gain = second_slope * spacing / (stamps[3] - stamps[1])
    weights = [-left_gain, first_base - right_gain, second_base + left_gain, right_gain]
    mine = []
    for offset in range(count):
        value = weights[offset]
        for start in range(count, 4, count):
            value = jnp.where(first == start, weights[start + offset], value)
        mine.append(value[0:1, :])
    return mine


def pack_kernel(sizes, parts, with_meta, *refs):
    (stored_ref, ids_ref, count_ref, snapshot_ref, between_ref, anchor_ref) = refs[:6]
    keep_ref, send_ref = refs[6:8]
    fields = refs[8 : 8 + len(parts)]
    sem = refs[8 + len(parts)]
    space_count, time_count, comp_count, snaps = sizes
    slots = ids_ref.shape[1]
    bricks_across = CXD * time_count // BRICK
    bricks_along = CY // BRICK
    bricks_deep = NZ // BRICK
    tile_bricks = bricks_across * bricks_along * bricks_deep
    capacity = tile_bricks // space_count
    span = ROWS * snaps
    copies = []
    for index, part in enumerate(parts):
        copy = pltpu.make_async_copy(
            stored_ref.at[:, pl.ds(part * span, span), :], fields[index], sem.at[index]
        )
        copy.start()
        copies.append(copy)
    space = lax.axis_index("space")
    comp = lax.axis_index("comp")
    time = lax.axis_index("tm")
    morton = ids_ref[...]
    slot = lax.broadcasted_iota(jnp.int32, (1, slots), 1)
    live = slot < count_ref[0]
    decoded = []
    for offset in (2, 1, 0):
        coordinate = jnp.zeros_like(morton)
        for level in range(GRID.bit_length() - 1):
            bit = lax.shift_right_logical(morton, 2 * level + offset) & (1 << level)
            coordinate = coordinate | bit
        decoded.append(coordinate)
    local_x = (decoded[0] - anchor_ref[0]) & (space_count * bricks_across - 1)
    local_y = (decoded[1] - anchor_ref[1]) & (comp_count * bricks_along - 1)
    local_z = (decoded[2] - anchor_ref[2]) & (bricks_deep - 1)
    hop = (local_x // bricks_across - space) & (space_count - 1)
    side = local_y // bricks_along
    place = local_z * (bricks_across * bricks_along) + (
        local_x % bricks_across
    ) * bricks_along + local_y % bricks_along
    label = jnp.where(live, hop * comp_count + side, -1)
    targets = space_count * comp_count
    tags = lax.broadcasted_iota(jnp.int32, (targets, slots), 0)
    member = jnp.where(tags == label, 1.0, 0.0)
    earlier = jnp.where(
        lax.broadcasted_iota(jnp.int32, (slots, slots), 0)
        < lax.broadcasted_iota(jnp.int32, (slots, slots), 1),
        1.0,
        0.0,
    ).astype(bf16)
    before = jnp.dot(member.astype(bf16), earlier, preferred_element_type=f32)
    rank = jnp.sum(before * member, axis=0, keepdims=True).astype(jnp.int32)
    position = jnp.where(comp == 0, rank, capacity - 1 - rank)
    key = jnp.where(live, hop * capacity + position, -1)
    mine = side == comp
    queue = lax.broadcasted_iota(jnp.int32, (tile_bricks, slots), 0)
    kept = jnp.where((queue == key) & mine, 1.0, 0.0).astype(bf16)
    sent = jnp.where((queue == key) & jnp.logical_not(mine), 1.0, 0.0).astype(bf16)
    onehot = jnp.concatenate([kept, sent], axis=0)
    base = len(parts) * ROWS * capacity
    if with_meta:
        hops = lax.broadcasted_iota(jnp.int32, (max(space_count, 8), slots), 0)
        labelled = jnp.where(hops == hop, place, 0).astype(f32).astype(bf16)
        for matrix, ref in ((kept, keep_ref), (sent, send_ref)):
            meta = lax.dot_general(
                labelled, matrix, (((1,), (1,)), ((), ())), preferred_element_type=f32
            )
            for step in range(space_count):
                ref[step, pl.ds(base, 8), :] = jnp.zeros((8, LANES), f32)
                for piece in range(tile_bricks // LANES):
                    ref[step, pl.ds(base + piece, 1), :] = meta[
                        step : step + 1, piece * LANES : (piece + 1) * LANES
                    ]
    weights = hermite_weights(snapshot_ref, between_ref, time * snaps, snaps)
    for index in range(len(parts)):
        copies[index].wait()
        flat = fields[index].reshape(slots * span, LANES)
        for row in range(ROWS):
            value = None
            for snap in range(snaps):
                term = weights[snap] * flat[pl.ds(row * snaps + snap, slots, stride=span), :]
                value = term if value is None else value + term
            rows = select_rows(onehot, value)
            for half, ref in ((0, keep_ref), (1, send_ref)):
                for step in range(space_count):
                    start = half * tile_bricks + step * capacity
                    ref[step, pl.ds((index * ROWS + row) * capacity, capacity), :] = rows[
                        start : start + capacity, :
                    ]


def swap_blocks(blocks):
    count = len(blocks)
    lane = lax.broadcasted_iota(jnp.int32, blocks[0].shape, 1)
    distance = 1
    while distance < count:
        shift = BRICK * distance
        upper = (lane & shift) != 0
        blocks = list(blocks)
        for index in range(count):
            if index & distance:
                continue
            first, second = blocks[index], blocks[index + distance]
            blocks[index] = jnp.where(upper, pltpu.roll(second, shift, 1), first)
            blocks[index + distance] = jnp.where(
                upper, second, pltpu.roll(first, LANES - shift, 1)
            )
        distance *= 2
    return blocks


def assemble_kernel(sizes, parts, wide, *refs):
    space_count, time_count, comp_count, _ = sizes
    bricks_across = CXD * time_count // BRICK
    bricks_along = CY // BRICK
    bricks_deep = NZ // BRICK
    stack = bricks_across * bricks_along
    tile_bricks = stack * bricks_deep
    capacity = tile_bricks // space_count
    messages = refs[:space_count]
    refs = refs[space_count:]
    if wide:
        places_ref, window_refs, edge_refs = (
            refs[0],
            refs[1 : 1 + time_count],
            refs[1 + time_count : 1 + 2 * time_count],
        )
        base = len(parts) * ROWS * capacity
        places = messages[0][pl.ds(base, 8), :]
        for message in messages[1:]:
            places = places + message[pl.ds(base, 8), :]
        places_ref[...] = places
    else:
        places = refs[0][...]
        window_refs = refs[1 : 1 + time_count]
    slab = refs[-1]
    place = jnp.concatenate(
        [places[piece : piece + 1, :] for piece in range(tile_bricks // LANES)], axis=1
    ).astype(jnp.int32)
    onehot = jnp.where(
        lax.broadcasted_iota(jnp.int32, (tile_bricks, tile_bricks), 0) == place, 1.0, 0.0
    ).astype(bf16)
    for index in range(len(parts)):
        for row in range(ROWS):
            queue = jnp.concatenate(
                [
                    message[pl.ds((index * ROWS + row) * capacity, capacity), :]
                    for message in messages
                ],
                axis=0,
            )
            rows = select_rows(onehot, queue)
            blocks = swap_blocks(
                [rows[deep * stack : (deep + 1) * stack, :] for deep in range(bricks_deep)]
            )
            for cell, block in enumerate(blocks):
                slab[
                    index, row * 2 + cell // BRICK, pl.ds(cell % BRICK, stack, stride=BRICK), :
                ] = block
    time = lax.axis_index("tm")
    own = CXD // BRICK
    for shift in range(time_count):
        target = lax.rem(time + shift, time_count)
        for index in range(len(parts)):
            for x in range(CXD):
                window_refs[shift][index, x] = slab[
                    index, x, pl.ds(pl.multiple_of(target * own * CY, CY), CY), :
                ]
            if wide:
                before, after = target - 1, target + 1
                if time_count == 2:
                    starts = ((jnp.where(target == 0, 0, REACH), 1 - target),)
                else:
                    starts = (
                        (CXD - REACH, jnp.maximum(before, 0)),
                        (0, jnp.minimum(after, time_count - 1)),
                    )
                for piece, (first, block) in enumerate(starts):
                    for x in range(REACH):
                        window_refs[shift][index, CXD + piece * REACH + x] = slab[
                            index, first + x, pl.ds(pl.multiple_of(block * CY, CY), CY), :
                        ]
    if wide:
        for order in range(time_count):
            last = time == order
            first = jnp.where(last, CXD - REACH, 0)
            block = jnp.where(last, bricks_across - 1, 0)
            for index in range(len(parts)):
                for x in range(REACH):
                    edge_refs[order][index, x] = slab[
                        index, first + x, pl.ds(pl.multiple_of(block * CY, CY), CY), :
                    ]


def difference(load):
    total = None
    for distance, coefficient in enumerate(coefficients, start=1):
        term = coefficient * (load(distance) - load(-distance))
        total = term if total is None else total + term
    return total


def along_z(value):
    def shifted(distance):
        return pltpu.roll(value, (-distance) % NZ, value.ndim - 1)

    return difference(shifted)


def curl_kernel(time_count, *refs):
    wide_refs = refs[:time_count]
    narrow_refs = refs[time_count : 2 * time_count]
    edge_refs = refs[2 * time_count : 3 * time_count]
    side_ref, out_ref, across, along = refs[3 * time_count :]

    def summed(group, *index):
        total = group[0][index]
        for ref in group[1:]:
            total = total + ref[index]
        return total

    time = lax.axis_index("tm")
    extra = 1 if time_count == 2 else 2
    for k in range(2):
        for x in range(CXD):
            value = summed(wide_refs, k, x)
            across[k, REACH + x] = value
            if k == 1:
                along[1, x, pl.ds(8, CY), :] = value
        for x in range(REACH):
            halo = summed(edge_refs, k, x)
            inner = summed(wide_refs, k, CXD + x)
            outer = summed(wide_refs, k, CXD + (extra - 1) * REACH + x)
            across[k, x] = jnp.where(time == 0, halo, inner)
            across[k, REACH + CXD + x] = jnp.where(time == time_count - 1, halo, outer)
    for x in range(CXD):
        along[0, x, pl.ds(8, CY), :] = summed(narrow_refs, 0, x)
        for k in range(2):
            along[k, x, pl.ds(0, 8), :] = side_ref[k, x, pl.ds(8, 8), :]
            along[k, x, pl.ds(8 + CY, 8), :] = side_ref[k, x, pl.ds(0, 8), :]
    for x in range(CXD):
        d_dy = [
            difference(lambda m, k=k: along[k, x, pl.ds(8 + m, CY), :]) for k in range(2)
        ]
        d_dx = [difference(lambda m, k=k: across[k, REACH + x + m]) for k in range(2)]
        u_z = along_z(along[0, x, pl.ds(8, CY), :])
        v_z = along_z(across[0, REACH + x])
        out_ref[0, x] = d_dy[1] - v_z
        out_ref[1, x] = u_z - d_dx[1]
        out_ref[2, x] = d_dx[0] - d_dy[0]


def body(stored, brick_ids, brick_counts, snapshot_ids, between, anchor):
    space_count = lax.axis_size("space")
    time_count = lax.axis_size("tm")
    comp_count = lax.axis_size("comp")
    slots, snaps = stored.shape[:2]
    sizes = (space_count, time_count, comp_count, snaps)
    tile_bricks = (CXD * time_count // BRICK) * (CY // BRICK) * (NZ // BRICK)
    capacity = tile_bricks // space_count
    span = ROWS * snaps
    cells = stored.transpose(0, 2, 1, 3).reshape(slots, 3, snaps, ROWS, LANES)
    cells = cells.transpose(0, 1, 3, 2, 4).reshape(slots, 3 * span, LANES)
    ids = brick_ids.reshape(1, slots)
    swap = [(i, comp_count - 1 - i) for i in range(comp_count)]

    def packed(parts, with_meta):
        rows = len(parts) * ROWS * capacity + (8 if with_meta else 0)
        shape = jax.ShapeDtypeStruct((space_count, rows, LANES), f32)
        keep, send = pl.pallas_call(
            functools.partial(pack_kernel, sizes, parts, with_meta),
            out_shape=(shape, shape),
            in_specs=[HBM, VMEM, SMEM, SMEM, SMEM, SMEM],
            out_specs=(VMEM, VMEM),
            scratch_shapes=[pltpu.VMEM((slots, span, LANES), f32) for _ in parts]
            + [pltpu.SemaphoreType.DMA((len(parts),))],
        )(cells, ids, brick_counts, snapshot_ids, between, anchor)
        other = lax.ppermute(send, "comp", swap)
        messages = []
        for hop in range(space_count):
            message = keep[hop] + other[hop]
            if hop > 0:
                ring = [(i, (i + hop) % space_count) for i in range(space_count)]
                message = lax.ppermute(message, "space", ring)
            messages.append(message)
        return messages

    def to_times(windows):
        moved = [windows[0]]
        for shift in range(1, time_count):
            ring = [(i, (i + shift) % time_count) for i in range(time_count)]
            moved.append(lax.ppermute(windows[shift], "tm", ring))
        return moved

    slab_rows = (CXD * time_count // BRICK) * CY
    wide_messages = packed((1, 2), True)
    narrow_messages = packed((0,), False)
    extent = CXD + (REACH if time_count == 2 else 2 * REACH)
    window = jax.ShapeDtypeStruct((2, extent, CY, NZ), f32)
    edge = jax.ShapeDtypeStruct((2, REACH, CY, NZ), f32)
    results = pl.pallas_call(
        functools.partial(assemble_kernel, sizes, (1, 2), True),
        out_shape=[jax.ShapeDtypeStruct((8, LANES), f32)]
        + [window] * time_count
        + [edge] * time_count,
        in_specs=[VMEM] * space_count,
        out_specs=[VMEM] * (1 + 2 * time_count),
        scratch_shapes=[pltpu.VMEM((2, CXD, slab_rows, NZ), f32)],
    )(*wide_messages)
    places = results[0]
    wide = to_times(results[1 : 1 + time_count])
    edges = []
    for order, value in enumerate(results[1 + time_count :]):
        pairs = []
        for s in range(space_count):
            pairs.append((s * time_count + order, (s + 1) % space_count * time_count))
            pairs.append(
                (
                    s * time_count + time_count - 1 - order,
                    (s - 1) % space_count * time_count + time_count - 1,
                )
            )
        edges.append(lax.ppermute(value, ("space", "tm"), pairs))
    small = jax.ShapeDtypeStruct((1, CXD, CY, NZ), f32)
    narrow = pl.pallas_call(
        functools.partial(assemble_kernel, sizes, (0,), False),
        out_shape=[small] * time_count,
        in_specs=[VMEM] * (space_count + 1),
        out_specs=[VMEM] * time_count,
        scratch_shapes=[pltpu.VMEM((1, CXD, slab_rows, NZ), f32)],
    )(*narrow_messages, places)
    narrow = to_times(narrow)

    def sides(group, k):
        low = sum(value[k, :CXD, :8] for value in group)
        high = sum(value[k, :CXD, CY - 8 :] for value in group)
        return jnp.concatenate([low, high], axis=1)

    side = jnp.stack([sides(narrow, 0), sides(wide, 1)])
    side = lax.ppermute(side, "comp", swap)
    return pl.pallas_call(
        functools.partial(curl_kernel, time_count),
        out_shape=jax.ShapeDtypeStruct((3, CXD, CY, NZ), f32),
        in_specs=[VMEM] * (3 * time_count + 1),
        out_specs=VMEM,
        scratch_shapes=[
            pltpu.VMEM((2, CXD + 2 * REACH, CY, NZ), f32),
            pltpu.VMEM((2, CXD, CY + 16, NZ), f32),
        ],
    )(*wide, *narrow, *edges, side)


def solution(mesh):
    return jax.shard_map(
        body,
        mesh=mesh,
        in_specs=(
            P(("groups", "space", "comp"), "tm", None, None),
            P(("groups", "space", "comp")),
            P(("groups", "space", "comp")),
            P("groups"),
            P("groups"),
            P("groups"),
        ),
        out_specs=P(None, ("groups", "space", "tm"), "comp", None),
        check_vma=False,
    )
```

time: 179 us -> 56.2 us (0.31); the launches traced: 175 us -> 55.6 us
  local copies, waits for them, and re-layouts: 59 us -> 1.97 us
  waiting for transfers between devices: 74.5 us -> 21.1 us
  between operations: 19 us -> 1.44 us
  Pallas kernels: 0 us -> 15.6 us
  other arithmetic: 8.58 us -> 4 us
  starting transfers between devices: 14.3 us -> 11.5 us
    all_to_all x2 -> x0, waiting for transfers between devices: 33 us -> none  [the longest x1 33 us: body(): lax.all_to_all(rows, ('space', 'comp'), split_axis=0, concat_axis=0, tile...]
    unnamed x30 -> x24, local copies, waits for them, and re-layouts: 21.9 us -> 1.97 us
    unnamed x3 -> x0, waiting for transfers between devices: 18.2 us -> none
    pallas_call x0 -> x5, Pallas kernels: none -> 15.6 us  [the longest x2 7.7 us: packed(): pl.pallas_call(functools.partial(pack_kernel, sizes, parts, with_meta), o...]
    reduce_scatter x1 -> x0, waiting for transfers between devices: 15.2 us -> none  [body(): lax.psum_scatter(weighted, 'tm', scatter_dimension=0, tiled=True)]
    scatter x3 -> x0, local copies, waits for them, and re-layouts: 13.3 us -> none  [the longest x1 7.56 us: body(): jnp.zeros((tile_bricks + 1,) + row_shape, jnp.float32).at[landing].set(rows)]
    ppermute x4 -> x13, waiting for transfers between devices: 8.12 us -> 21.1 us  [the longest x2 10.8 us: to_times(): moved.append(lax.ppermute(windows[shift], 'tm', ring))]
    slice x19 -> x0, local copies, waits for them, and re-layouts: 11.8 us -> none  [the longest x2 6.2 us: body(): weighted = mine[0] * stored[:, 0]]
  transfers between devices with their start and end apart: 8 -> 13, of which waited for: 7 -> 4; matrix products, arithmetic and copies ran while one was open for 9% -> 7% of each run, Pallas kernels for 0% -> 16%
where the time goes in v1:
time: 56.2 us; the launch traced here: 55.6 us
  waiting for transfers between devices  21.1 us (38%)
  Pallas kernels  15.6 us (28%)
  starting transfers between devices  11.5 us (20%)
  other arithmetic  4 us (7%)
  local copies, waits for them, and re-layouts  1.97 us (4%)
  between operations  1.44 us (3%)
    ppermute x2, waiting for transfers between devices, to_times(): moved.append(lax.ppermute(windows[shift], 'tm', ring))  10.8 us
    ppermute x6, waiting for transfers between devices, packed(): message = lax.ppermute(message, 'space', ring)  9.38 us
    pallas_call x2, Pallas kernels, packed(): pl.pallas_call(functools.partial(pack_kernel, sizes, parts, with_meta), o...  7.7 us
    ppermute x6, starting transfers between devices, packed(): message = lax.ppermute(message, 'space', ring)  6.93 us
    pallas_call x1, Pallas kernels, body(): pl.pallas_call(functools.partial(assemble_kernel, sizes, (1, 2), True), o...  2.96 us
    pallas_call x1, Pallas kernels, body(): pl.pallas_call(functools.partial(curl_kernel, time_count), out_shape=jax....  2.69 us
    add x2, other arithmetic, packed(): message = keep[hop] + other[hop]  2.29 us
    pallas_call x1, Pallas kernels, body(): pl.pallas_call(functools.partial(assemble_kernel, sizes, (0,), False), ou...  2.24 us
  transfers between devices with their start and end apart: 13, of which 4 were waited for; matrix products, arithmetic and copies ran while one was open for 7% of the time, Pallas kernels for 16%

profile of v1, /device:TPU:11, one launch (start us, length us, event | category | flops | bytes accessed | tf_op | source)
XLA Modules:
  0.0 55.6 jit_solution(10348229384072060839)
XLA Ops:
  1.3 4.3 %shard_map.64 = (f32[4,264,128]{2,1,0:T(8,128)}, f32[4,264,128]{2,1,0:T(8,128)}) custom-call(f32[256,24,128]{2,1,0:T(8,128)} %bitcast.36, s32[1,256]{1,0:T(1,128)} %bitcast.38, s32[1]{0:T(128)S(6)} %copy.8.refs_2_, s32[4]{0:T(128)} %refs_3_.3, f32[1]{0:T(128)S(6)} %copy.9.refs_4_, s32[3]{0:T(128)} %refs_5_.3), custom_call_target="tpu_custom_call" | custom-call | tf_op jit(solution)/shard_map/pallas_call | solution.py:337
  5.6 0.0 copy-start
  5.6 0.7 %collective-permute-start = (f32[4,264,128]{2,1,0:T(8,128)}, f32[4,264,128]{2,1,0:T(8,128)S(1)}, u32[]{:S(2)}, u32[]{:S(2)}) collective-permute-start(f32[4,264,128]{2,1,0:T(8,128)} %get-tuple-element.17), channel_id=1, source_target_pairs={{0,1},{1,0},{2,3},{3,2},{4,5},{5,4},{6,7},{7,6},{8,9},{9,8},{10,11... | collective-permute-start | bytes 1622024 | tf_op jit(solution)/shard_map/ppermute | solution.py:345
  6.3 3.4 %shard_map.66 = (f32[4,128,128]{2,1,0:T(8,128)}, f32[4,128,128]{2,1,0:T(8,128)}) custom-call(f32[256,24,128]{2,1,0:T(8,128)} %bitcast.37, s32[1,256]{1,0:T(1,128)} %bitcast.39, s32[1]{0:T(128)S(6)} %copy.8.refs_2_, s32[4]{0:T(128)} %refs_3_.3, f32[1]{0:T(128)S(6)} %copy.9.refs_4_, s32[3]{0:T(128)} %refs_5_.3), custom_call_target="tpu_custom_call" | custom-call | tf_op jit(solution)/shard_map/pallas_call | solution.py:337
  9.8 0.1 collective-permute-start.5
  9.8 0.0 collective-permute-done
  9.9 0.0 copy-done
  9.9 0.7 %fusion = (f32[264,128]{1,0:T(8,128)S(1)}, f32[264,128]{1,0:T(8,128)S(1)}, f32[264,128]{1,0:T(8,128)S(1)}, f32[264,128]{1,0:T(8,128)}) fusion(f32[4,264,128]{2,1,0:T(8,128)S(1)} %collective-permute-done, f32[4,264,128]{2,1,0:T(8,128)S(1)} %copy-done), kind=kLoop, calls=%fused_computation.1 | loop fusion | flops 135168 | bytes 1622016 | tf_op jit(solution)/shard_map/add | solution.py:348
  10.6 1.3 %collective-permute-start.1 = (f32[264,128]{1,0:T(8,128)S(1)}, f32[264,128]{1,0:T(8,128)S(1)}, u32[]{:S(2)}, u32[]{:S(2)}) collective-permute-start(f32[264,128]{1,0:T(8,128)S(1)} %get-tuple-element.29), channel_id=1, source_target_pairs={{0,4},{4,8},{8,12},{12,0},{1,5},{5,9},{9,13},{13,1},{2,6},{6,10},{... | collective-permute-start | bytes 405512 | tf_op jit(solution)/shard_map/ppermute | solution.py:351
  11.9 1.0 %collective-permute-start.2 = (f32[264,128]{1,0:T(8,128)S(1)}, f32[264,128]{1,0:T(8,128)S(1)}, u32[]{:S(2)}, u32[]{:S(2)}) collective-permute-start(f32[264,128]{1,0:T(8,128)S(1)} %get-tuple-element.28), channel_id=1, source_target_pairs={{0,8},{4,12},{8,0},{12,4},{1,9},{5,13},{9,1},{13,5},{2,10},{6,14},... | collective-permute-start | bytes 405512 | tf_op jit(solution)/shard_map/ppermute | solution.py:351
  12.9 1.5 %collective-permute-start.3 = (f32[264,128]{1,0:T(8,128)S(1)}, f32[264,128]{1,0:T(8,128)S(1)}, u32[]{:S(2)}, u32[]{:S(2)}) collective-permute-start(f32[264,128]{1,0:T(8,128)S(1)} %get-tuple-element.27), channel_id=1, source_target_pairs={{0,12},{4,0},{8,4},{12,8},{1,13},{5,1},{9,5},{13,9},{2,14},{6,2},{... | collective-permute-start | bytes 405512 | tf_op jit(solution)/shard_map/ppermute | solution.py:351
  14.3 0.0 collective-permute-done.5
  14.4 1.6 %fusion.4 = (f32[128,128]{1,0:T(8,128)S(1)}, f32[128,128]{1,0:T(8,128)S(1)}, f32[128,128]{1,0:T(8,128)S(1)}, f32[128,128]{1,0:T(8,128)}) fusion(f32[4,128,128]{2,1,0:T(8,128)S(1)} %collective-permute-done.5, f32[4,128,128]{2,1,0:T(8,128)} %get-tuple-element.20), kind=kLoop, calls=%fused_computation.10 | loop fusion | flops 65536 | bytes 786432 | tf_op jit(solution)/shard_map/add | solution.py:348
  15.9 0.0 collective-permute-start.6
  15.9 3.1 %collective-permute-start.7 = (f32[128,128]{1,0:T(8,128)S(1)}, f32[128,128]{1,0:T(8,128)S(1)}, u32[]{:S(2)}, u32[]{:S(2)}) collective-permute-start(f32[128,128]{1,0:T(8,128)S(1)} %get-tuple-element.34), channel_id=1, source_target_pairs={{0,8},{4,12},{8,0},{12,4},{1,9},{5,13},{9,1},{13,5},{2,10},{6,14},... | collective-permute-start | bytes 196616 | tf_op jit(solution)/shard_map/ppermute | solution.py:351
  19.1 0.0 collective-permute-done.1.refs_1_
  19.1 0.0 collective-permute-start.8
  19.1 6.6 %collective-permute-done.2.refs_2_ = f32[264,128]{1,0:T(8,128)S(1)} collective-permute-done((f32[264,128]{1,0:T(8,128)S(1)}, f32[264,128]{1,0:T(8,128)S(1)}, u32[]{:S(2)}, u32[]{:S(2)}) %collective-permute-start.2) | collective-permute-done | bytes 135200 | tf_op jit(solution)/shard_map/ppermute | solution.py:351
  25.7 2.8 %collective-permute-done.3.refs_3_ = f32[264,128]{1,0:T(8,128)S(1)} collective-permute-done((f32[264,128]{1,0:T(8,128)S(1)}, f32[264,128]{1,0:T(8,128)S(1)}, u32[]{:S(2)}, u32[]{:S(2)}) %collective-permute-start.3) | collective-permute-done | bytes 135200 | tf_op jit(solution)/shard_map/ppermute | solution.py:351
  28.5 0.0 copy-done.3
  28.5 0.0 copy-done.4
  28.5 0.7 %copy-done.5 = f32[264,128]{1,0:T(8,128)} copy-done((f32[264,128]{1,0:T(8,128)}, f32[264,128]{1,0:T(8,128)S(1)}, u32[]{:S(2)}) %copy-start.5) | copy-done | bytes 135192
  29.1 3.0 %shard_map.65 = (f32[8,128]{1,0:T(8,128)}, f32[2,12,32,128]{3,2,1,0:T(8,128)}, f32[2,12,32,128]{3,2,1,0:T(8,128)}, f32[2,4,32,128]{3,2,1,0:T(8,128)}, f32[2,4,32,128]{3,2,1,0:T(8,128)}) custom-call(f32[264,128]{1,0:T(8,128)} %get-tuple-element.30.refs_0_, f32[264,128]{1,0:T(8,128)} %copy-done.3, f32[264,128]{1,0:T(8,128)} %copy-done.4, f32[264,128]{1,0:T(8,128)} %copy-done.5), custom_call_target="tpu_custom_call" | custom-call | tf_op jit(solution)/shard_map/pallas_call | solution.py:368
  32.1 0.2 collective-permute-start.4
  32.3 0.0 collective-permute-done.6.refs_1_
  32.3 0.0 collective-permute-done.7.refs_2_
  32.4 0.0 copy-start.10
  32.4 0.0 collective-permute-done.8.refs_3_
  32.4 0.6 %copy-done.9 = f32[128,128]{1,0:T(8,128)} copy-done((f32[128,128]{1,0:T(8,128)}, f32[128,128]{1,0:T(8,128)S(1)}, u32[]{:S(2)}) %copy-start.9) | copy-done | bytes 65560
  33.0 0.0 copy-done.10
  33.0 0.0 copy-done.11
  33.0 2.2 %shard_map.67 = (f32[1,8,32,128]{3,2,1,0:T(8,128)}, f32[1,8,32,128]{3,2,1,0:T(8,128)}) custom-call(f32[128,128]{1,0:T(8,128)} %get-tuple-element.36.refs_0_, f32[128,128]{1,0:T(8,128)} %copy-done.9, f32[128,128]{1,0:T(8,128)} %copy-done.10, f32[128,128]{1,0:T(8,128)} %copy-done.11, f32[8,128]{1,0:T(8,128)} %get-tuple-element.22.refs_4_), custom_call_target="tpu_custom_call" | custom-call | tf_op jit(solution)/shard_map/pallas_call | solution.py:392
  35.3 1.2 %collective-permute-start.9 = (f32[1,8,32,128]{3,2,1,0:T(8,128)}, f32[1,8,32,128]{3,2,1,0:T(8,128)S(1)}, u32[]{:S(2)}, u32[]{:S(2)}) collective-permute-start(f32[1,8,32,128]{3,2,1,0:T(8,128)} %get-tuple-element.24), channel_id=1, source_target_pairs={{0,2},{2,0},{1,3},{3,1},{4,6},{6,4},{5,7},{7,5},{8,10},{10,8},{9,1... | collective-permute-start | bytes 393224 | tf_op jit(solution)/shard_map/ppermute | solution.py:359
  36.5 0.0 collective-permute-start.10
  36.5 0.8 %collective-permute-start.11 = (f32[2,4,32,128]{3,2,1,0:T(8,128)}, f32[2,4,32,128]{3,2,1,0:T(8,128)S(1)}, u32[]{:S(2)}, u32[]{:S(2)}) collective-permute-start(f32[2,4,32,128]{3,2,1,0:T(8,128)} %get-tuple-element.26), channel_id=1, source_target_pairs={{2,4},{0,14},{6,8},{4,2},{10,12},{8,6},{14,0},{12,10},{3,5},{1,15}... | collective-permute-start | bytes 393224 | tf_op jit(solution)/shard_map/ppermute | solution.py:390
  37.3 10.8 %collective-permute-done.9.refs_3_ = f32[1,8,32,128]{3,2,1,0:T(8,128)S(1)} collective-permute-done((f32[1,8,32,128]{3,2,1,0:T(8,128)}, f32[1,8,32,128]{3,2,1,0:T(8,128)S(1)}, u32[]{:S(2)}, u32[]{:S(2)}) %collective-permute-start.9) | collective-permute-done | bytes 131104 | tf_op jit(solution)/shard_map/ppermute | solution.py:359
  48.0 0.8 %fusion.11 = (f32[8,8,128]{2,1,0:T(8,128)S(1)}, f32[8,8,128]{2,1,0:T(8,128)S(1)}) fusion(f32[1,8,32,128]{3,2,1,0:T(8,128)S(1)} %collective-permute-done.9.refs_3_, f32[1,8,32,128]{3,2,1,0:T(8,128)} %get-tuple-element.23.refs_2_), kind=kLoop, calls=%fused_computation.26 | loop fusion | flops 16384 | bytes 196608 | tf_op jit(solution)/shard_map/add | solution.py:402
  48.8 0.0 collective-permute-done.4.refs_1_
  48.9 0.0 copy-start.1
  48.9 0.9 %fusion.9 = (f32[8,8,128]{2,1,0:T(8,128)S(1)}, f32[8,8,128]{2,1,0:T(8,128)S(1)}) fusion(f32[2,12,32,128]{3,2,1,0:T(8,128)S(1)} %collective-permute-done.4.refs_1_, f32[2,12,32,128]{3,2,1,0:T(8,128)} %get-tuple-element.18.refs_0_), kind=kLoop, calls=%fused_computation.22 | loop fusion | flops 16384 | bytes 196608 | tf_op jit(solution)/shard_map/add | solution.py:402
  49.8 1.5 %collective-permute-start.12 = (f32[2,8,16,128]{3,2,1,0:T(8,128)S(1)}, f32[2,8,16,128]{3,2,1,0:T(8,128)S(1)}, u32[]{:S(2)}, u32[]{:S(2)}) collective-permute-start(f32[2,8,16,128]{3,2,1,0:T(8,128)S(1)} %pad_maximum_fusion), channel_id=1, source_target_pairs={{0,1},{1,0},{2,3},{3,2},{4,5},{5,4},{6,7},{7,6},{8,9},{9,8},{10,11... | collective-permute-start | bytes 393224 | tf_op jit(solution)/shard_map/ppermute | solution.py:407
  51.3 0.0 collective-permute-done.10.refs_4_
  51.3 0.0 collective-permute-done.11.refs_5_
  51.3 1.0 %collective-permute-done.12.refs_6_ = f32[2,8,16,128]{3,2,1,0:T(8,128)S(1)} collective-permute-done((f32[2,8,16,128]{3,2,1,0:T(8,128)S(1)}, f32[2,8,16,128]{3,2,1,0:T(8,128)S(1)}, u32[]{:S(2)}, u32[]{:S(2)}) %collective-permute-start.12) | collective-permute-done | bytes 131104 | tf_op jit(solution)/shard_map/ppermute | solution.py:407
  52.3 0.0 copy-done.2
  52.3 0.0 copy-start.8
  52.3 0.6 %copy-done.8 = f32[2,8,16,128]{3,2,1,0:T(8,128)} copy-done((f32[2,8,16,128]{3,2,1,0:T(8,128)}, f32[2,8,16,128]{3,2,1,0:T(8,128)S(1)}, u32[]{:S(2)}) %copy-start.8) | copy-done | bytes 131096
  52.9 2.7 %shard_map.68 = f32[3,8,32,128]{3,2,1,0:T(8,128)} custom-call(f32[2,12,32,128]{3,2,1,0:T(8,128)} %get-tuple-element.18.refs_0_, f32[2,12,32,128]{3,2,1,0:T(8,128)} %copy-done.1, f32[1,8,32,128]{3,2,1,0:T(8,128)} %get-tuple-element.23.refs_2_, f32[1,8,32,128]{3,2,1,0:T(8,128)} %copy-done.2, f32[2,4,32,128]{3,2,1,0:T(8,128)} %copy-done.6, ...), custom_call_target="tpu_custom_call" | custom-call | tf_op jit(solution)/shard_map/pallas_call | solution.py:408
  (13 shorter events, 0.0 us)
Async XLA Ops:
  5.6 4.3 %copy-start = (f32[4,264,128]{2,1,0:T(8,128)S(1)}, f32[4,264,128]{2,1,0:T(8,128)}, u32[]{:S(2)}) copy-start(f32[4,264,128]{2,1,0:T(8,128)} %get-tuple-element.16) | copy-start | bytes 1622020
  5.6 4.3 %collective-permute-start = (f32[4,264,128]{2,1,0:T(8,128)}, f32[4,264,128]{2,1,0:T(8,128)S(1)}, u32[]{:S(2)}, u32[]{:S(2)}) collective-permute-start(f32[4,264,128]{2,1,0:T(8,128)} %get-tuple-element.17), channel_id=1, source_target_pairs={{0,1},{1,0},{2,3},{3,2},{4,5},{5,4},{6,7},{7,6},{8,9},{9,8},{10,11... | collective-permute-start | bytes 1622024 | tf_op jit(solution)/shard_map/ppermute | solution.py:345
  9.8 4.6 %collective-permute-start.5 = (f32[4,128,128]{2,1,0:T(8,128)}, f32[4,128,128]{2,1,0:T(8,128)S(1)}, u32[]{:S(2)}, u32[]{:S(2)}) collective-permute-start(f32[4,128,128]{2,1,0:T(8,128)} %get-tuple-element.21), channel_id=1, source_target_pairs={{0,1},{1,0},{2,3},{3,2},{4,5},{5,4},{6,7},{7,6},{8,9},{9,8},{10,11... | collective-permute-start | bytes 786440 | tf_op jit(solution)/shard_map/ppermute | solution.py:345
  10.6 8.5 %collective-permute-start.1 = (f32[264,128]{1,0:T(8,128)S(1)}, f32[264,128]{1,0:T(8,128)S(1)}, u32[]{:S(2)}, u32[]{:S(2)}) collective-permute-start(f32[264,128]{1,0:T(8,128)S(1)} %get-tuple-element.29), channel_id=1, source_target_pairs={{0,4},{4,8},{8,12},{12,0},{1,5},{5,9},{9,13},{13,1},{2,6},{6,10},{... | collective-permute-start | bytes 405512 | tf_op jit(solution)/shard_map/ppermute | solution.py:351
  11.9 13.8 %collective-permute-start.2 = (f32[264,128]{1,0:T(8,128)S(1)}, f32[264,128]{1,0:T(8,128)S(1)}, u32[]{:S(2)}, u32[]{:S(2)}) collective-permute-start(f32[264,128]{1,0:T(8,128)S(1)} %get-tuple-element.28), channel_id=1, source_target_pairs={{0,8},{4,12},{8,0},{12,4},{1,9},{5,13},{9,1},{13,5},{2,10},{6,14},... | collective-permute-start | bytes 405512 | tf_op jit(solution)/shard_map/ppermute | solution.py:351
  12.9 15.6 %collective-permute-start.3 = (f32[264,128]{1,0:T(8,128)S(1)}, f32[264,128]{1,0:T(8,128)S(1)}, u32[]{:S(2)}, u32[]{:S(2)}) collective-permute-start(f32[264,128]{1,0:T(8,128)S(1)} %get-tuple-element.27), channel_id=1, source_target_pairs={{0,12},{4,0},{8,4},{12,8},{1,13},{5,1},{9,5},{13,9},{2,14},{6,2},{... | collective-permute-start | bytes 405512 | tf_op jit(solution)/shard_map/ppermute | solution.py:351
  15.9 16.4 %collective-permute-start.6 = (f32[128,128]{1,0:T(8,128)S(1)}, f32[128,128]{1,0:T(8,128)S(1)}, u32[]{:S(2)}, u32[]{:S(2)}) collective-permute-start(f32[128,128]{1,0:T(8,128)S(1)} %get-tuple-element.35), channel_id=1, source_target_pairs={{0,4},{4,8},{8,12},{12,0},{1,5},{5,9},{9,13},{13,1},{2,6},{6,10},{... | collective-permute-start | bytes 196616 | tf_op jit(solution)/shard_map/ppermute | solution.py:351
  15.9 16.4 %collective-permute-start.7 = (f32[128,128]{1,0:T(8,128)S(1)}, f32[128,128]{1,0:T(8,128)S(1)}, u32[]{:S(2)}, u32[]{:S(2)}) collective-permute-start(f32[128,128]{1,0:T(8,128)S(1)} %get-tuple-element.34), channel_id=1, source_target_pairs={{0,8},{4,12},{8,0},{12,4},{1,9},{5,13},{9,1},{13,5},{2,10},{6,14},... | collective-permute-start | bytes 196616 | tf_op jit(solution)/shard_map/ppermute | solution.py:351
  19.1 9.4 %copy-start.3 = (f32[264,128]{1,0:T(8,128)}, f32[264,128]{1,0:T(8,128)S(1)}, u32[]{:S(2)}) copy-start(f32[264,128]{1,0:T(8,128)S(1)} %collective-permute-done.1.refs_1_) | copy-start | bytes 405508
  19.1 13.3 %collective-permute-start.8 = (f32[128,128]{1,0:T(8,128)S(1)}, f32[128,128]{1,0:T(8,128)S(1)}, u32[]{:S(2)}, u32[]{:S(2)}) collective-permute-start(f32[128,128]{1,0:T(8,128)S(1)} %get-tuple-element.33), channel_id=1, source_target_pairs={{0,12},{4,0},{8,4},{12,8},{1,13},{5,1},{9,5},{13,9},{2,14},{6,2},{... | collective-permute-start | bytes 196616 | tf_op jit(solution)/shard_map/ppermute | solution.py:351
  25.7 2.8 %copy-start.4 = (f32[264,128]{1,0:T(8,128)}, f32[264,128]{1,0:T(8,128)S(1)}, u32[]{:S(2)}) copy-start(f32[264,128]{1,0:T(8,128)S(1)} %collective-permute-done.2.refs_2_) | copy-start | bytes 405508
  28.5 0.7 %copy-start.5 = (f32[264,128]{1,0:T(8,128)}, f32[264,128]{1,0:T(8,128)S(1)}, u32[]{:S(2)}) copy-start(f32[264,128]{1,0:T(8,128)S(1)} %collective-permute-done.3.refs_3_) | copy-start | bytes 405508
  32.1 16.8 %collective-permute-start.4 = (f32[2,12,32,128]{3,2,1,0:T(8,128)}, f32[2,12,32,128]{3,2,1,0:T(8,128)S(1)}, u32[]{:S(2)}, u32[]{:S(2)}) collective-permute-start(f32[2,12,32,128]{3,2,1,0:T(8,128)} %get-tuple-element.19), channel_id=1, source_target_pairs={{0,2},{2,0},{1,3},{3,1},{4,6},{6,4},{5,7},{7,5},{8,10},{10,8},{9,1... | collective-permute-start | bytes 1179656 | tf_op jit(solution)/shard_map/ppermute | solution.py:359
  32.3 0.6 %copy-start.9 = (f32[128,128]{1,0:T(8,128)}, f32[128,128]{1,0:T(8,128)S(1)}, u32[]{:S(2)}) copy-start(f32[128,128]{1,0:T(8,128)S(1)} %collective-permute-done.6.refs_1_) | copy-start | bytes 196612
  32.4 0.6 %copy-start.10 = (f32[128,128]{1,0:T(8,128)}, f32[128,128]{1,0:T(8,128)S(1)}, u32[]{:S(2)}) copy-start(f32[128,128]{1,0:T(8,128)S(1)} %collective-permute-done.7.refs_2_) | copy-start | bytes 196612
  32.4 0.6 %copy-start.11 = (f32[128,128]{1,0:T(8,128)}, f32[128,128]{1,0:T(8,128)S(1)}, u32[]{:S(2)}) copy-start(f32[128,128]{1,0:T(8,128)S(1)} %collective-permute-done.8.refs_3_) | copy-start | bytes 196612
  35.3 12.7 %collective-permute-start.9 = (f32[1,8,32,128]{3,2,1,0:T(8,128)}, f32[1,8,32,128]{3,2,1,0:T(8,128)S(1)}, u32[]{:S(2)}, u32[]{:S(2)}) collective-permute-start(f32[1,8,32,128]{3,2,1,0:T(8,128)} %get-tuple-element.24), channel_id=1, source_target_pairs={{0,2},{2,0},{1,3},{3,1},{4,6},{6,4},{5,7},{7,5},{8,10},{10,8},{9,1... | collective-permute-start | bytes 393224 | tf_op jit(solution)/shard_map/ppermute | solution.py:359
  36.5 14.8 %collective-permute-start.10 = (f32[2,4,32,128]{3,2,1,0:T(8,128)}, f32[2,4,32,128]{3,2,1,0:T(8,128)S(1)}, u32[]{:S(2)}, u32[]{:S(2)}) collective-permute-start(f32[2,4,32,128]{3,2,1,0:T(8,128)} %get-tuple-element.25), channel_id=1, source_target_pairs={{0,4},{2,14},{4,8},{6,2},{8,12},{10,6},{12,0},{14,10},{1,5},{3,15}... | collective-permute-start | bytes 393224 | tf_op jit(solution)/shard_map/ppermute | solution.py:390
  36.5 14.8 %collective-permute-start.11 = (f32[2,4,32,128]{3,2,1,0:T(8,128)}, f32[2,4,32,128]{3,2,1,0:T(8,128)S(1)}, u32[]{:S(2)}, u32[]{:S(2)}) collective-permute-start(f32[2,4,32,128]{3,2,1,0:T(8,128)} %get-tuple-element.26), channel_id=1, source_target_pairs={{2,4},{0,14},{6,8},{4,2},{10,12},{8,6},{14,0},{12,10},{3,5},{1,15}... | collective-permute-start | bytes 393224 | tf_op jit(solution)/shard_map/ppermute | solution.py:390
  48.0 4.3 %copy-start.2 = (f32[1,8,32,128]{3,2,1,0:T(8,128)}, f32[1,8,32,128]{3,2,1,0:T(8,128)S(1)}, u32[]{:S(2)}) copy-start(f32[1,8,32,128]{3,2,1,0:T(8,128)S(1)} %collective-permute-done.9.refs_3_) | copy-start | bytes 393220
  48.9 3.4 %copy-start.1 = (f32[2,12,32,128]{3,2,1,0:T(8,128)}, f32[2,12,32,128]{3,2,1,0:T(8,128)S(1)}, u32[]{:S(2)}) copy-start(f32[2,12,32,128]{3,2,1,0:T(8,128)S(1)} %collective-permute-done.4.refs_1_) | copy-start | bytes 1179652
  49.8 2.5 %collective-permute-start.12 = (f32[2,8,16,128]{3,2,1,0:T(8,128)S(1)}, f32[2,8,16,128]{3,2,1,0:T(8,128)S(1)}, u32[]{:S(2)}, u32[]{:S(2)}) collective-permute-start(f32[2,8,16,128]{3,2,1,0:T(8,128)S(1)} %pad_maximum_fusion), channel_id=1, source_target_pairs={{0,1},{1,0},{2,3},{3,2},{4,5},{5,4},{6,7},{7,6},{8,9},{9,8},{10,11... | collective-permute-start | bytes 393224 | tf_op jit(solution)/shard_map/ppermute | solution.py:407
  51.3 1.0 %copy-start.6 = (f32[2,4,32,128]{3,2,1,0:T(8,128)}, f32[2,4,32,128]{3,2,1,0:T(8,128)S(1)}, u32[]{:S(2)}) copy-start(f32[2,4,32,128]{3,2,1,0:T(8,128)S(1)} %collective-permute-done.10.refs_4_) | copy-start | bytes 393220
  51.3 1.0 %copy-start.7 = (f32[2,4,32,128]{3,2,1,0:T(8,128)}, f32[2,4,32,128]{3,2,1,0:T(8,128)S(1)}, u32[]{:S(2)}) copy-start(f32[2,4,32,128]{3,2,1,0:T(8,128)S(1)} %collective-permute-done.11.refs_5_) | copy-start | bytes 393220
  52.3 0.7 %copy-start.8 = (f32[2,8,16,128]{3,2,1,0:T(8,128)}, f32[2,8,16,128]{3,2,1,0:T(8,128)S(1)}, u32[]{:S(2)}) copy-start(f32[2,8,16,128]{3,2,1,0:T(8,128)S(1)} %collective-permute-done.12.refs_6_) | copy-start | bytes 393220

commit v2 on v1

--- a/solution.py
+++ b/solution.py
@@ -6,6 +6,7 @@
 from jax.experimental import pallas as pl
 from jax.experimental.pallas import tpu as pltpu
 from jax.sharding import PartitionSpec as P
+
 
 BRICK = 8
 GRID = 1024
@@ -16,13 +17,15 @@
 ROWS = BRICK**3 // LANES
 REACH = 4
 
+
 coefficients = (0.8, -0.2, 4.0 / 105.0, -1.0 / 280.0)
 
 VMEM = pl.BlockSpec(memory_space=pltpu.VMEM)
 SMEM = pl.BlockSpec(memory_space=pltpu.SMEM)
-HBM = pl.BlockSpec(memory_space=pl.ANY)
+HBM = pl.BlockSpec(memory_space=pltpu.HBM)
 f32 = jnp.float32
 bf16 = jnp.bfloat16
+LIMIT = pltpu.CompilerParams(vmem_limit_bytes=16 * 1024 * 1024)
 
 
 def thirds(value):
@@ -64,11 +67,28 @@
     return mine
 
 
-def pack_kernel(sizes, parts, with_meta, *refs):
-    (stored_ref, ids_ref, count_ref, snapshot_ref, between_ref, anchor_ref) = refs[:6]
-    keep_ref, send_ref = refs[6:8]
-    fields = refs[8 : 8 + len(parts)]
-    sem = refs[8 + len(parts)]
+def pack_rows(sizes, index, load, weights, onehot, refs):
+    space_count, _, _, snaps = sizes
+    tile_bricks = onehot.shape[0] // len(refs)
+    capacity = tile_bricks // space_count
+    for row in range(ROWS):
+        value = None
+        for snap in range(snaps):
+            term = weights[snap] * load(row * snaps + snap)
+            value = term if value is None else value + term
+        rows = select_rows(onehot, value)
+        for half, ref in enumerate(refs):
+            for step in range(space_count):
+                start = half * tile_bricks + step * capacity
+                ref[step, pl.ds((index * ROWS + row) * capacity, capacity), :] = rows[
+                    start : start + capacity, :
+                ]
+
+
+def pack_kernel(sizes, *refs):
+    stored_ref, ids_hbm, snapshot_hbm, anchor_hbm, count_ref, between_ref = refs[:6]
+    keep_ref, send_ref, later_ref, onehot_ref, weights_ref = refs[6:11]
+    first_ref, second_ref, ids_ref, snapshot_ref, anchor_ref, sem = refs[11:]
     space_count, time_count, comp_count, snaps = sizes
     slots = ids_ref.shape[1]
     bricks_across = CXD * time_count // BRICK
@@ -77,16 +97,29 @@
     tile_bricks = bricks_across * bricks_along * bricks_deep
     capacity = tile_bricks // space_count
     span = ROWS * snaps
-    copies = []
-    for index, part in enumerate(parts):
-        copy = pltpu.make_async_copy(
-            stored_ref.at[:, pl.ds(part * span, span), :], fields[index], sem.at[index]
-        )
+    pairs = [(ids_hbm, ids_ref), (snapshot_hbm, snapshot_ref), (anchor_hbm, anchor_ref)]
+    for part, field in ((1, first_ref), (2, second_ref), (0, later_ref)):
+        pairs.append((stored_ref.at[:, pl.ds(part * span, span), :], field))
+    copies = [
+        pltpu.make_async_copy(source, target, sem.at[index])
+        for index, (source, target) in enumerate(pairs)
+    ]
+    for copy in copies:
         copy.start()
-        copies.append(copy)
     space = lax.axis_index("space")
     comp = lax.axis_index("comp")
     time = lax.axis_index("tm")
+    earlier = jnp.where(
+        lax.broadcasted_iota(jnp.int32, (slots, slots), 0)
+        < lax.broadcasted_iota(jnp.int32, (slots, slots), 1),
+        1.0,
+        0.0,
+    ).astype(bf16)
+    for copy in copies[:3]:
+        copy.wait()
+    weights = hermite_weights(snapshot_ref, between_ref, time * snaps, snaps)
+    for snap in range(snaps):
+        weights_ref[pl.ds(snap, 1), :] = weights[snap]
     morton = ids_ref[...]
     slot = lax.broadcasted_iota(jnp.int32, (1, slots), 1)
     live = slot < count_ref[0]
@@ -100,60 +133,66 @@
     local_x = (decoded[0] - anchor_ref[0]) & (space_count * bricks_across - 1)
     local_y = (decoded[1] - anchor_ref[1]) & (comp_count * bricks_along - 1)
     local_z = (decoded[2] - anchor_ref[2]) & (bricks_deep - 1)
-    hop = (local_x // bricks_across - space) & (space_count - 1)
+    hop = (local_x // bricks_across) ^ space
     side = local_y // bricks_along
     place = local_z * (bricks_across * bricks_along) + (
         local_x % bricks_across
     ) * bricks_along + local_y % bricks_along
     label = jnp.where(live, hop * comp_count + side, -1)
-    targets = space_count * comp_count
-    tags = lax.broadcasted_iota(jnp.int32, (targets, slots), 0)
+    tags = lax.broadcasted_iota(jnp.int32, (space_count * comp_count, slots), 0)
     member = jnp.where(tags == label, 1.0, 0.0)
-    earlier = jnp.where(
-        lax.broadcasted_iota(jnp.int32, (slots, slots), 0)
-        < lax.broadcasted_iota(jnp.int32, (slots, slots), 1),
-        1.0,
-        0.0,
-    ).astype(bf16)
     before = jnp.dot(member.astype(bf16), earlier, preferred_element_type=f32)
     rank = jnp.sum(before * member, axis=0, keepdims=True).astype(jnp.int32)
     position = jnp.where(comp == 0, rank, capacity - 1 - rank)
     key = jnp.where(live, hop * capacity + position, -1)
     mine = side == comp
+    kept_key = jnp.where(mine, key, -1)
+    sent_key = jnp.where(mine, -1, key)
     queue = lax.broadcasted_iota(jnp.int32, (tile_bricks, slots), 0)
-    kept = jnp.where((queue == key) & mine, 1.0, 0.0).astype(bf16)
-    sent = jnp.where((queue == key) & jnp.logical_not(mine), 1.0, 0.0).astype(bf16)
+    kept = jnp.where(queue == kept_key, 1.0, 0.0).astype(bf16)
+    sent = jnp.where(queue == sent_key, 1.0, 0.0).astype(bf16)
     onehot = jnp.concatenate([kept, sent], axis=0)
-    base = len(parts) * ROWS * capacity
-    if with_meta:
-        hops = lax.broadcasted_iota(jnp.int32, (max(space_count, 8), slots), 0)
-        labelled = jnp.where(hops == hop, place, 0).astype(f32).astype(bf16)
-        for matrix, ref in ((kept, keep_ref), (sent, send_ref)):
-            meta = lax.dot_general(
-                labelled, matrix, (((1,), (1,)), ((), ())), preferred_element_type=f32
-            )
-            for step in range(space_count):
-                ref[step, pl.ds(base, 8), :] = jnp.zeros((8, LANES), f32)
-                for piece in range(tile_bricks // LANES):
-                    ref[step, pl.ds(base + piece, 1), :] = meta[
-                        step : step + 1, piece * LANES : (piece + 1) * LANES
-                    ]
-    weights = hermite_weights(snapshot_ref, between_ref, time * snaps, snaps)
-    for index in range(len(parts)):
-        copies[index].wait()
-        flat = fields[index].reshape(slots * span, LANES)
-        for row in range(ROWS):
-            value = None
-            for snap in range(snaps):
-                term = weights[snap] * flat[pl.ds(row * snaps + snap, slots, stride=span), :]
-                value = term if value is None else value + term
-            rows = select_rows(onehot, value)
-            for half, ref in ((0, keep_ref), (1, send_ref)):
-                for step in range(space_count):
-                    start = half * tile_bricks + step * capacity
-                    ref[step, pl.ds((index * ROWS + row) * capacity, capacity), :] = rows[
-                        start : start + capacity, :
-                    ]
+    onehot_ref[...] = onehot
+    base = 2 * ROWS * capacity
+    hops = lax.broadcasted_iota(jnp.int32, (max(space_count, 8), slots), 0)
+    labelled = jnp.where(hops == hop, place, 0).astype(f32).astype(bf16)
+    metas = lax.dot_general(
+        labelled, onehot, (((1,), (1,)), ((), ())), preferred_element_type=f32
+    )
+    for half, ref in ((0, keep_ref), (1, send_ref)):
+        for step in range(space_count):
+            ref[step, pl.ds(base, 8), :] = jnp.zeros((8, LANES), f32)
+            for piece in range(tile_bricks // LANES):
+                start = half * tile_bricks + piece * LANES
+                ref[step, pl.ds(base + piece, 1), :] = metas[
+                    step : step + 1, start : start + LANES
+                ]
+    for index, field in enumerate((first_ref, second_ref)):
+        copies[3 + index].wait()
+        flat = field.reshape(slots * span, LANES)
+        pack_rows(
+            sizes,
+            index,
+            lambda row, flat=flat: flat[pl.ds(row, slots, stride=span), :],
+            weights,
+            onehot,
+            (keep_ref, send_ref),
+        )
+    copies[5].wait()
+
+
+def pack_later_kernel(sizes, field_ref, onehot_ref, weights_ref, keep_ref, send_ref):
+    snaps = sizes[3]
+    slots, span = field_ref.shape[:2]
+    flat = field_ref.reshape(slots * span, LANES)
+    pack_rows(
+        sizes,
+        0,
+        lambda row: flat[pl.ds(row, slots, stride=span), :],
+        [weights_ref[pl.ds(snap, 1), :] for snap in range(snaps)],
+        onehot_ref[...],
+        (keep_ref, send_ref),
+    )
 
 
 def swap_blocks(blocks):
@@ -177,7 +216,7 @@
 
 
 def assemble_kernel(sizes, parts, wide, *refs):
-    space_count, time_count, comp_count, _ = sizes
+    space_count, time_count, _, _ = sizes
     bricks_across = CXD * time_count // BRICK
     bricks_along = CY // BRICK
     bricks_deep = NZ // BRICK
@@ -199,7 +238,7 @@
         places_ref[...] = places
     else:
         places = refs[0][...]
-        window_refs = refs[1 : 1 + time_count]
+        window_refs = refs[1:2]
     slab = refs[-1]
     place = jnp.concatenate(
         [places[piece : piece + 1, :] for piece in range(tile_bricks // LANES)], axis=1
@@ -226,7 +265,7 @@
                 ] = block
     time = lax.axis_index("tm")
     own = CXD // BRICK
-    for shift in range(time_count):
+    for shift in range(len(window_refs)):
         target = lax.rem(time + shift, time_count)
         for index in range(len(parts)):
             for x in range(CXD):
@@ -248,15 +287,19 @@
                             index, first + x, pl.ds(pl.multiple_of(block * CY, CY), CY), :
                         ]
     if wide:
-        for order in range(time_count):
-            last = time == order
+        for shift in range(time_count):
+            last = lax.rem(time + shift, time_count) == 0
             first = jnp.where(last, CXD - REACH, 0)
             block = jnp.where(last, bricks_across - 1, 0)
             for index in range(len(parts)):
                 for x in range(REACH):
-                    edge_refs[order][index, x] = slab[
+                    edge_refs[shift][index, x] = slab[
                         index, first + x, pl.ds(pl.multiple_of(block * CY, CY), CY), :
                     ]
+
+
+def own_kernel(*refs):
+    refs[-1][...] = sum(ref[0] for ref in refs[:-1])
 
 
 def difference(load):
@@ -276,9 +319,8 @@
 
 def curl_kernel(time_count, *refs):
     wide_refs = refs[:time_count]
-    narrow_refs = refs[time_count : 2 * time_count]
-    edge_refs = refs[2 * time_count : 3 * time_count]
-    side_ref, out_ref, across, along = refs[3 * time_count :]
+    narrow_ref = refs[time_count]
+    edge_ref, narrow_side_ref, wide_side_ref, out_ref, across, along = refs[time_count + 1 :]
 
     def summed(group, *index):
         total = group[0][index]
@@ -295,16 +337,16 @@
             if k == 1:
                 along[1, x, pl.ds(8, CY), :] = value
         for x in range(REACH):
-            halo = summed(edge_refs, k, x)
+            halo = edge_ref[k, x]
             inner = summed(wide_refs, k, CXD + x)
             outer = summed(wide_refs, k, CXD + (extra - 1) * REACH + x)
             across[k, x] = jnp.where(time == 0, halo, inner)
             across[k, REACH + CXD + x] = jnp.where(time == time_count - 1, halo, outer)
     for x in range(CXD):
-        along[0, x, pl.ds(8, CY), :] = summed(narrow_refs, 0, x)
-        for k in range(2):
-            along[k, x, pl.ds(0, 8), :] = side_ref[k, x, pl.ds(8, 8), :]
-            along[k, x, pl.ds(8 + CY, 8), :] = side_ref[k, x, pl.ds(0, 8), :]
+        along[0, x, pl.ds(8, CY), :] = narrow_ref[0, x]
+        for k, ref in enumerate((narrow_side_ref, wide_side_ref)):
+            along[k, x, pl.ds(0, 8), :] = ref[x, pl.ds(8, 8), :]
+            along[k, x, pl.ds(8 + CY, 8), :] = ref[x, pl.ds(0, 8), :]
     for x in range(CXD):
         d_dy = [
             difference(lambda m, k=k: along[k, x, pl.ds(8 + m, CY), :]) for k in range(2)
@@ -323,45 +365,74 @@
     comp_count = lax.axis_size("comp")
     slots, snaps = stored.shape[:2]
     sizes = (space_count, time_count, comp_count, snaps)
-    tile_bricks = (CXD * time_count // BRICK) * (CY // BRICK) * (NZ // BRICK)
+    bricks_across = CXD * time_count // BRICK
+    tile_bricks = bricks_across * (CY // BRICK) * (NZ // BRICK)
     capacity = tile_bricks // space_count
     span = ROWS * snaps
     cells = stored.transpose(0, 2, 1, 3).reshape(slots, 3, snaps, ROWS, LANES)
     cells = cells.transpose(0, 1, 3, 2, 4).reshape(slots, 3 * span, LANES)
     ids = brick_ids.reshape(1, slots)
+    held = [
+        pltpu.with_memory_space_constraint(value, pltpu.HBM)
+        for value in (cells, ids, snapshot_ids, anchor)
+    ]
     swap = [(i, comp_count - 1 - i) for i in range(comp_count)]
 
-    def packed(parts, with_meta):
-        rows = len(parts) * ROWS * capacity + (8 if with_meta else 0)
-        shape = jax.ShapeDtypeStruct((space_count, rows, LANES), f32)
-        keep, send = pl.pallas_call(
-            functools.partial(pack_kernel, sizes, parts, with_meta),
-            out_shape=(shape, shape),
-            in_specs=[HBM, VMEM, SMEM, SMEM, SMEM, SMEM],
-            out_specs=(VMEM, VMEM),
-            scratch_shapes=[pltpu.VMEM((slots, span, LANES), f32) for _ in parts]
-            + [pltpu.SemaphoreType.DMA((len(parts),))],
-        )(cells, ids, brick_counts, snapshot_ids, between, anchor)
-        other = lax.ppermute(send, "comp", swap)
-        messages = []
-        for hop in range(space_count):
-            message = keep[hop] + other[hop]
-            if hop > 0:
-                ring = [(i, (i + hop) % space_count) for i in range(space_count)]
-                message = lax.ppermute(message, "space", ring)
-            messages.append(message)
-        return messages
+    def to_places(messages):
+        moved = [messages[0]]
+        for hop in range(1, space_count):
+            ring = [(i, i ^ hop) for i in range(space_count)]
+            moved.append(lax.ppermute(messages[hop], "space", ring))
+        return moved
 
     def to_times(windows):
         moved = [windows[0]]
         for shift in range(1, time_count):
             ring = [(i, (i + shift) % time_count) for i in range(time_count)]
-            moved.append(lax.ppermute(windows[shift], "tm", ring))
+            value = windows[shift % len(windows)]
+            moved.append(lax.ppermute(value, "tm", ring))
         return moved
 
-    slab_rows = (CXD * time_count // BRICK) * CY
-    wide_messages = packed((1, 2), True)
-    narrow_messages = packed((0,), False)
+    wide_rows = 2 * ROWS * capacity + 8
+    field = (slots, span, LANES)
+    wide_shape = jax.ShapeDtypeStruct((space_count, wide_rows, LANES), f32)
+    keep, send, later, onehot, weights = pl.pallas_call(
+        functools.partial(pack_kernel, sizes),
+        out_shape=(
+            wide_shape,
+            wide_shape,
+            jax.ShapeDtypeStruct(field, f32),
+            jax.ShapeDtypeStruct((2 * tile_bricks, slots), bf16),
+            jax.ShapeDtypeStruct((8, LANES), f32),
+        ),
+        in_specs=[HBM] * 4 + [SMEM] * 2,
+        out_specs=(VMEM,) * 5,
+        scratch_shapes=[
+            pltpu.VMEM(field, f32),
+            pltpu.VMEM(field, f32),
+            pltpu.VMEM(ids.shape, jnp.int32),
+            pltpu.SMEM(snapshot_ids.shape, jnp.int32),
+            pltpu.SMEM(anchor.shape, jnp.int32),
+            pltpu.SemaphoreType.DMA((6,)),
+        ],
+        compiler_params=LIMIT,
+    )(*held, brick_counts, between)
+    other = lax.ppermute(send, "comp", swap)
+    wide_messages = to_places([keep[hop] + other[hop] for hop in range(space_count)])
+
+    narrow_shape = jax.ShapeDtypeStruct((space_count, ROWS * capacity, LANES), f32)
+    keep, send = pl.pallas_call(
+        functools.partial(pack_later_kernel, sizes),
+        out_shape=(narrow_shape,) * 2,
+        in_specs=[VMEM] * 3,
+        out_specs=(VMEM,) * 2,
+        compiler_params=LIMIT,
+    )(later, onehot, weights)
+    partial = keep + lax.ppermute(send, "comp", swap)
+    shares = to_times([partial])
+    whole = [sum(share[hop] for share in shares) for hop in range(1, space_count)]
+
+    slab_rows = bricks_across * CY
     extent = CXD + (REACH if time_count == 2 else 2 * REACH)
     window = jax.ShapeDtypeStruct((2, extent, CY, NZ), f32)
     edge = jax.ShapeDtypeStruct((2, REACH, CY, NZ), f32)
@@ -373,48 +444,52 @@
         in_specs=[VMEM] * space_count,
         out_specs=[VMEM] * (1 + 2 * time_count),
         scratch_shapes=[pltpu.VMEM((2, CXD, slab_rows, NZ), f32)],
+        compiler_params=LIMIT,
     )(*wide_messages)
+    whole, results = lax.optimization_barrier((whole, results))
     places = results[0]
+    edge = to_times(results[1 + time_count :])
+    edge = sum(edge[1:], edge[0])
     wide = to_times(results[1 : 1 + time_count])
-    edges = []
-    for order, value in enumerate(results[1 + time_count :]):
-        pairs = []
-        for s in range(space_count):
-            pairs.append((s * time_count + order, (s + 1) % space_count * time_count))
-            pairs.append(
-                (
-                    s * time_count + time_count - 1 - order,
-                    (s - 1) % space_count * time_count + time_count - 1,
-                )
-            )
-        edges.append(lax.ppermute(value, ("space", "tm"), pairs))
-    small = jax.ShapeDtypeStruct((1, CXD, CY, NZ), f32)
+    pairs = []
+    for s in range(space_count):
+        pairs.append((s * time_count, (s + 1) % space_count * time_count))
+        last = time_count - 1
+        pairs.append((s * time_count + last, (s - 1) % space_count * time_count + last))
+    edge = lax.ppermute(edge, ("space", "tm"), pairs)
+    own = pl.pallas_call(
+        own_kernel,
+        out_shape=jax.ShapeDtypeStruct(partial.shape[1:], f32),
+        in_specs=[VMEM] * time_count,
+        out_specs=VMEM,
+        compiler_params=LIMIT,
+    )(*shares)
+    narrow_messages = to_places([own, *whole])
     narrow = pl.pallas_call(
         functools.partial(assemble_kernel, sizes, (0,), False),
-        out_shape=[small] * time_count,
+        out_shape=[jax.ShapeDtypeStruct((1, CXD, CY, NZ), f32)],
         in_specs=[VMEM] * (space_count + 1),
-        out_specs=[VMEM] * time_count,
+        out_specs=[VMEM],
         scratch_shapes=[pltpu.VMEM((1, CXD, slab_rows, NZ), f32)],
+        compiler_params=LIMIT,
     )(*narrow_messages, places)
-    narrow = to_times(narrow)
 
     def sides(group, k):
         low = sum(value[k, :CXD, :8] for value in group)
         high = sum(value[k, :CXD, CY - 8 :] for value in group)
-        return jnp.concatenate([low, high], axis=1)
-
-    side = jnp.stack([sides(narrow, 0), sides(wide, 1)])
-    side = lax.ppermute(side, "comp", swap)
+        return lax.ppermute(jnp.concatenate([low, high], axis=1), "comp", swap)
+
     return pl.pallas_call(
         functools.partial(curl_kernel, time_count),
         out_shape=jax.ShapeDtypeStruct((3, CXD, CY, NZ), f32),
-        in_specs=[VMEM] * (3 * time_count + 1),
+        in_specs=[VMEM] * (time_count + 4),
         out_specs=VMEM,
         scratch_shapes=[
             pltpu.VMEM((2, CXD + 2 * REACH, CY, NZ), f32),
             pltpu.VMEM((2, CXD, CY + 16, NZ), f32),
         ],
-    )(*wide, *narrow, *edges, side)
+        compiler_params=LIMIT,
+    )(*wide, *narrow, edge, sides(narrow, 0), sides(wide, 1))
 
 
 def solution(mesh):

time: 56.2 us -> 50.8 us (0.904)
  the two profiles are of different devices: /device:TPU:11 before, /device:TPU:0 now
where the time goes in v2:
time: 50.8 us; the launch traced here: 50.6 us
  waiting for transfers between devices  28.5 us (56%)
  starting transfers between devices  14.5 us (29%)
  Pallas kernels  6.05 us (12%)
  between operations  1.42 us (3%)
    ppermute x6, waiting for transfers between devices, to_places(): moved.append(lax.ppermute(messages[hop], 'space', ring))  11.2 us
    ppermute x3, waiting for transfers between devices, to_times(): moved.append(lax.ppermute(value, 'tm', ring))  9.1 us
    ppermute x6, starting transfers between devices, to_places(): moved.append(lax.ppermute(messages[hop], 'space', ring))  8.89 us
    ppermute x1, waiting for transfers between devices, body(): edge = lax.ppermute(edge, ('space', 'tm'), pairs)  6.62 us
    ppermute x3, starting transfers between devices, to_times(): moved.append(lax.ppermute(value, 'tm', ring))  4.77 us
    pallas_call x1, Pallas kernels, body(): pl.pallas_call(functools.partial(pack_kernel, sizes), out_shape=(wide_sha...  2.53 us
    ppermute x1, waiting for transfers between devices, body(): partial = keep + lax.ppermute(send, 'comp', swap)  1.52 us
    pallas_call x1, Pallas kernels, body(): pl.pallas_call(functools.partial(curl_kernel, time_count), out_shape=jax....  1.39 us
  transfers between devices with their start and end apart: 14, of which 8 were waited for; matrix products, arithmetic and copies ran while one was open for 0% of the time, Pallas kernels for 2%

profile of v2, /device:TPU:0, one launch (start us, length us, event | category | flops | bytes accessed | tf_op | source)
XLA Modules:
  0.0 50.6 jit_solution(6249556526703933918)
XLA Ops:
  1.3 2.5 %shard_map.64 = (f32[4,264,128]{2,1,0:T(8,128)S(1)}, f32[4,264,128]{2,1,0:T(8,128)S(1)}, f32[256,8,128]{2,1,0:T(8,128)S(1)}, bf16[256,256]{1,0:T(8,128)(2,1)S(1)}, f32[8,128]{1,0:T(8,128)S(1)}) custom-call(f32[256,24,128]{2,1,0:T(8,128)} %bitcast.30, s32[1,256]{1,0:T(1,128)} %bitcast.31, s32[4]{0:T(128)} %refs_2_.1, s32[3]{0:T(128)} %refs_3_.1, ...), custom_call_target="tpu_custom_call" | custom-call | tf_op jit(solution)/shard_map/pallas_call | solution.py:399
  3.8 0.6 %collective-permute-start.2 = (f32[4,264,128]{2,1,0:T(8,128)S(1)}, f32[4,264,128]{2,1,0:T(8,128)S(1)}, u32[]{:S(2)}, u32[]{:S(2)}) collective-permute-start(f32[4,264,128]{2,1,0:T(8,128)S(1)} %get-tuple-element.31), channel_id=1, source_target_pairs={{0,1},{1,0},{2,3},{3,2},{4,5},{5,4},{6,7},{7,6},{8,9},{9,8},{10,11... | collective-permute-start | bytes 1622024 | tf_op jit(solution)/shard_map/ppermute | solution.py:420
  4.4 0.6 %shard_map.65 = (f32[4,128,128]{2,1,0:T(8,128)S(1)}, f32[4,128,128]{2,1,0:T(8,128)S(1)}) custom-call(f32[256,8,128]{2,1,0:T(8,128)S(1)} %get-tuple-element.25.field_ref, bf16[256,256]{1,0:T(8,128)(2,1)S(1)} %get-tuple-element.26.onehot_ref, f32[8,128]{1,0:T(8,128)S(1)} %get-tuple-element.27.weights_ref), custom_call_target="tpu_custom_call" | custom-call | tf_op jit(solution)/shard_map/pallas_call | solution.py:424
  5.0 0.1 collective-permute-start
  5.1 1.5 %collective-permute-done = f32[4,128,128]{2,1,0:T(8,128)S(1)} collective-permute-done((f32[4,128,128]{2,1,0:T(8,128)S(1)}, f32[4,128,128]{2,1,0:T(8,128)S(1)}, u32[]{:S(2)}, u32[]{:S(2)}) %collective-permute-start) | collective-permute-done | bytes 262176 | tf_op jit(solution)/shard_map/ppermute | solution.py:431
  6.6 2.7 %collective-permute-start.1 = (f32[4,128,128]{2,1,0:T(8,128)S(1)}, f32[4,128,128]{2,1,0:T(8,128)S(1)}, u32[]{:S(2)}, u32[]{:S(2)}) collective-permute-start(f32[4,128,128]{2,1,0:T(8,128)S(1)} %add.59.refs_0_), channel_id=1, source_target_pairs={{0,2},{2,0},{1,3},{3,1},{4,6},{6,4},{5,7},{7,5},{8,10},{10,8},{9,1... | collective-permute-start | bytes 786440 | tf_op jit(solution)/shard_map/ppermute | solution.py:393
  9.3 0.0 collective-permute-done.2
  9.3 0.1 fusion
  9.4 3.7 %collective-permute-start.5 = (f32[264,128]{1,0:T(8,128)S(1)}, f32[264,128]{1,0:T(8,128)S(1)}, u32[]{:S(2)}, u32[]{:S(2)}) collective-permute-start(f32[264,128]{1,0:T(8,128)S(1)} %get-tuple-element.45), channel_id=1, source_target_pairs={{0,12},{4,8},{8,4},{12,0},{1,13},{5,9},{9,5},{13,1},{2,14},{6,10},... | collective-permute-start | bytes 405512 | tf_op jit(solution)/shard_map/ppermute | solution.py:385
  13.1 0.0 collective-permute-start.4
  13.1 0.8 %collective-permute-start.3 = (f32[264,128]{1,0:T(8,128)S(1)}, f32[264,128]{1,0:T(8,128)S(1)}, u32[]{:S(2)}, u32[]{:S(2)}) collective-permute-start(f32[264,128]{1,0:T(8,128)S(1)} %get-tuple-element.47), channel_id=1, source_target_pairs={{0,4},{4,0},{8,12},{12,8},{1,5},{5,1},{9,13},{13,9},{2,6},{6,2},{1... | collective-permute-start | bytes 405512 | tf_op jit(solution)/shard_map/ppermute | solution.py:385
  13.9 2.3 %collective-permute-done.1.refs_1_ = f32[4,128,128]{2,1,0:T(8,128)S(1)} collective-permute-done((f32[4,128,128]{2,1,0:T(8,128)S(1)}, f32[4,128,128]{2,1,0:T(8,128)S(1)}, u32[]{:S(2)}, u32[]{:S(2)}) %collective-permute-start.1) | collective-permute-done | bytes 262176 | tf_op jit(solution)/shard_map/ppermute | solution.py:393
  16.2 1.6 %collective-permute-done.5.refs_3_ = f32[264,128]{1,0:T(8,128)S(1)} collective-permute-done((f32[264,128]{1,0:T(8,128)S(1)}, f32[264,128]{1,0:T(8,128)S(1)}, u32[]{:S(2)}, u32[]{:S(2)}) %collective-permute-start.5) | collective-permute-done | bytes 135200 | tf_op jit(solution)/shard_map/ppermute | solution.py:385
  17.8 6.9 %collective-permute-done.4.refs_2_ = f32[264,128]{1,0:T(8,128)S(1)} collective-permute-done((f32[264,128]{1,0:T(8,128)S(1)}, f32[264,128]{1,0:T(8,128)S(1)}, u32[]{:S(2)}, u32[]{:S(2)}) %collective-permute-start.4) | collective-permute-done | bytes 135200 | tf_op jit(solution)/shard_map/ppermute | solution.py:385
  24.8 0.0 collective-permute-done.3.refs_1_
  24.8 0.9 %shard_map.66 = (f32[8,128]{1,0:T(8,128)S(1)}, f32[2,12,32,128]{3,2,1,0:T(8,128)S(1)}, f32[2,12,32,128]{3,2,1,0:T(8,128)S(1)}, f32[2,4,32,128]{3,2,1,0:T(8,128)S(1)}, f32[2,4,32,128]{3,2,1,0:T(8,128)S(1)}) custom-call(f32[264,128]{1,0:T(8,128)S(1)} %get-tuple-element.48.refs_0_, f32[264,128]{1,0:T(8,128)S(1)} %collective-permute-done.3.refs_1_, ...), custom_call_target="tpu_custom_call" | custom-call | tf_op jit(solution)/shard_map/pallas_call | solution.py:439
  25.7 0.1 collective-permute-start.7
  25.8 3.1 %collective-permute-start.8 = (f32[128,128]{1,0:T(8,128)S(1)}, f32[128,128]{1,0:T(8,128)S(1)}, u32[]{:S(2)}, u32[]{:S(2)}) collective-permute-start(f32[128,128]{1,0:T(8,128)S(1)} %get-tuple-element.40), channel_id=1, source_target_pairs={{0,8},{4,12},{8,0},{12,4},{1,9},{5,13},{9,1},{13,5},{2,10},{6,14},... | collective-permute-start | bytes 196616 | tf_op jit(solution)/shard_map/ppermute | solution.py:385
  28.8 1.3 %collective-permute-start.9 = (f32[128,128]{1,0:T(8,128)S(1)}, f32[128,128]{1,0:T(8,128)S(1)}, u32[]{:S(2)}, u32[]{:S(2)}) collective-permute-start(f32[128,128]{1,0:T(8,128)S(1)} %get-tuple-element.41), channel_id=1, source_target_pairs={{0,12},{4,8},{8,4},{12,0},{1,13},{5,9},{9,5},{13,1},{2,14},{6,10},... | collective-permute-start | bytes 196616 | tf_op jit(solution)/shard_map/ppermute | solution.py:385
  30.2 0.5 %collective-permute-start.6 = (f32[2,12,32,128]{3,2,1,0:T(8,128)S(1)}, f32[2,12,32,128]{3,2,1,0:T(8,128)S(1)}, u32[]{:S(2)}, u32[]{:S(2)}) collective-permute-start(f32[2,12,32,128]{3,2,1,0:T(8,128)S(1)} %get-tuple-element.38), channel_id=1, source_target_pairs={{0,2},{2,0},{1,3},{3,1},{4,6},{6,4},{5,7},{7,5},{8,10},{10,8},{9,1... | collective-permute-start | bytes 1179656 | tf_op jit(solution)/shard_map/ppermute | solution.py:393
  30.7 1.6 %collective-permute-start.10 = (f32[2,4,32,128]{3,2,1,0:T(8,128)S(1)}, f32[2,4,32,128]{3,2,1,0:T(8,128)S(1)}, u32[]{:S(2)}, u32[]{:S(2)}) collective-permute-start(f32[2,4,32,128]{3,2,1,0:T(8,128)S(1)} %get-tuple-element.44), channel_id=1, source_target_pairs={{0,2},{2,0},{1,3},{3,1},{4,6},{6,4},{5,7},{7,5},{8,10},{10,8},{9,1... | collective-permute-start | bytes 393224 | tf_op jit(solution)/shard_map/ppermute | solution.py:393
  32.3 0.0 collective-permute-done.7.refs_1_
  32.3 1.0 %collective-permute-done.8.refs_2_ = f32[128,128]{1,0:T(8,128)S(1)} collective-permute-done((f32[128,128]{1,0:T(8,128)S(1)}, f32[128,128]{1,0:T(8,128)S(1)}, u32[]{:S(2)}, u32[]{:S(2)}) %collective-permute-start.8) | collective-permute-done | bytes 65568 | tf_op jit(solution)/shard_map/ppermute | solution.py:385
  33.2 1.7 %collective-permute-done.9.refs_3_ = f32[128,128]{1,0:T(8,128)S(1)} collective-permute-done((f32[128,128]{1,0:T(8,128)S(1)}, f32[128,128]{1,0:T(8,128)S(1)}, u32[]{:S(2)}, u32[]{:S(2)}) %collective-permute-start.9) | collective-permute-done | bytes 65568 | tf_op jit(solution)/shard_map/ppermute | solution.py:385
  34.9 0.6 %shard_map.68.refs_2_ = f32[1,8,32,128]{3,2,1,0:T(8,128)S(1)} custom-call(f32[128,128]{1,0:T(8,128)S(1)} %shard_map.67.refs_0_, f32[128,128]{1,0:T(8,128)S(1)} %collective-permute-done.7.refs_1_, f32[128,128]{1,0:T(8,128)S(1)} %collective-permute-done.8.refs_2_, f32[128,128]{1,0:T(8,128)S(1)} %collective-permute-done.9.refs_3_, ...), custom_call_target="tpu_custom_call" | custom-call | tf_op jit(solution)/shard_map/pallas_call | solution.py:468
  35.5 0.1 collective-permute-start.12
  35.6 6.8 %collective-permute-done.10 = f32[2,4,32,128]{3,2,1,0:T(8,128)S(1)} collective-permute-done((f32[2,4,32,128]{3,2,1,0:T(8,128)S(1)}, f32[2,4,32,128]{3,2,1,0:T(8,128)S(1)}, u32[]{:S(2)}, u32[]{:S(2)}) %collective-permute-start.10) | collective-permute-done | bytes 131104 | tf_op jit(solution)/shard_map/ppermute | solution.py:393
  42.4 0.1 collective-permute-start.11
  42.5 0.0 collective-permute-done.6.refs_1_
  42.5 0.1 collective-permute-start.13
  42.6 0.0 collective-permute-done.12.refs_4_
  42.6 6.6 %collective-permute-done.11.refs_3_ = f32[2,4,32,128]{3,2,1,0:T(8,128)S(1)} collective-permute-done((f32[2,4,32,128]{3,2,1,0:T(8,128)S(1)}, f32[2,4,32,128]{3,2,1,0:T(8,128)S(1)}, u32[]{:S(2)}, u32[]{:S(2)}) %collective-permute-start.11) | collective-permute-done | bytes 131104 | tf_op jit(solution)/shard_map/ppermute | solution.py:459
  49.2 0.0 collective-permute-done.13.refs_5_
  49.2 1.4 %shard_map.69 = f32[3,8,32,128]{3,2,1,0:T(8,128)} custom-call(f32[2,12,32,128]{3,2,1,0:T(8,128)S(1)} %get-tuple-element.37.refs_0_, f32[2,12,32,128]{3,2,1,0:T(8,128)S(1)} %collective-permute-done.6.refs_1_, f32[1,8,32,128]{3,2,1,0:T(8,128)S(1)} %shard_map.68.refs_2_, f32[2,4,32,128]{3,2,1,0:T(8,128)S(1)} %collective-permute-done.11.refs_3_, ...), custom_call_target="tpu_custom_call" | custom-call | tf_op jit(solution)/shard_map/pallas_call | solution.py:482
  (8 shorter events, 0.1 us)
Async XLA Ops:
  3.8 5.5 %collective-permute-start.2 = (f32[4,264,128]{2,1,0:T(8,128)S(1)}, f32[4,264,128]{2,1,0:T(8,128)S(1)}, u32[]{:S(2)}, u32[]{:S(2)}) collective-permute-start(f32[4,264,128]{2,1,0:T(8,128)S(1)} %get-tuple-element.31), channel_id=1, source_target_pairs={{0,1},{1,0},{2,3},{3,2},{4,5},{5,4},{6,7},{7,6},{8,9},{9,8},{10,11... | collective-permute-start | bytes 1622024 | tf_op jit(solution)/shard_map/ppermute | solution.py:420
  5.0 1.6 %collective-permute-start = (f32[4,128,128]{2,1,0:T(8,128)S(1)}, f32[4,128,128]{2,1,0:T(8,128)S(1)}, u32[]{:S(2)}, u32[]{:S(2)}) collective-permute-start(f32[4,128,128]{2,1,0:T(8,128)S(1)} %get-tuple-element.29), channel_id=1, source_target_pairs={{0,1},{1,0},{2,3},{3,2},{4,5},{5,4},{6,7},{7,6},{8,9},{9,8},{10,11... | collective-permute-start | bytes 786440 | tf_op jit(solution)/shard_map/ppermute | solution.py:431
  6.6 9.5 %collective-permute-start.1 = (f32[4,128,128]{2,1,0:T(8,128)S(1)}, f32[4,128,128]{2,1,0:T(8,128)S(1)}, u32[]{:S(2)}, u32[]{:S(2)}) collective-permute-start(f32[4,128,128]{2,1,0:T(8,128)S(1)} %add.59.refs_0_), channel_id=1, source_target_pairs={{0,2},{2,0},{1,3},{3,1},{4,6},{6,4},{5,7},{7,5},{8,10},{10,8},{9,1... | collective-permute-start | bytes 786440 | tf_op jit(solution)/shard_map/ppermute | solution.py:393
  9.4 8.4 %collective-permute-start.5 = (f32[264,128]{1,0:T(8,128)S(1)}, f32[264,128]{1,0:T(8,128)S(1)}, u32[]{:S(2)}, u32[]{:S(2)}) collective-permute-start(f32[264,128]{1,0:T(8,128)S(1)} %get-tuple-element.45), channel_id=1, source_target_pairs={{0,12},{4,8},{8,4},{12,0},{1,13},{5,9},{9,5},{13,1},{2,14},{6,10},... | collective-permute-start | bytes 405512 | tf_op jit(solution)/shard_map/ppermute | solution.py:385
  13.1 11.7 %collective-permute-start.4 = (f32[264,128]{1,0:T(8,128)S(1)}, f32[264,128]{1,0:T(8,128)S(1)}, u32[]{:S(2)}, u32[]{:S(2)}) collective-permute-start(f32[264,128]{1,0:T(8,128)S(1)} %get-tuple-element.46), channel_id=1, source_target_pairs={{0,8},{4,12},{8,0},{12,4},{1,9},{5,13},{9,1},{13,5},{2,10},{6,14},... | collective-permute-start | bytes 405512 | tf_op jit(solution)/shard_map/ppermute | solution.py:385
  13.1 11.7 %collective-permute-start.3 = (f32[264,128]{1,0:T(8,128)S(1)}, f32[264,128]{1,0:T(8,128)S(1)}, u32[]{:S(2)}, u32[]{:S(2)}) collective-permute-start(f32[264,128]{1,0:T(8,128)S(1)} %get-tuple-element.47), channel_id=1, source_target_pairs={{0,4},{4,0},{8,12},{12,8},{1,5},{5,1},{9,13},{13,9},{2,6},{6,2},{1... | collective-permute-start | bytes 405512 | tf_op jit(solution)/shard_map/ppermute | solution.py:385
  25.7 6.6 %collective-permute-start.7 = (f32[128,128]{1,0:T(8,128)S(1)}, f32[128,128]{1,0:T(8,128)S(1)}, u32[]{:S(2)}, u32[]{:S(2)}) collective-permute-start(f32[128,128]{1,0:T(8,128)S(1)} %get-tuple-element.39), channel_id=1, source_target_pairs={{0,4},{4,0},{8,12},{12,8},{1,5},{5,1},{9,13},{13,9},{2,6},{6,2},{1... | collective-permute-start | bytes 196616 | tf_op jit(solution)/shard_map/ppermute | solution.py:385
  25.8 7.5 %collective-permute-start.8 = (f32[128,128]{1,0:T(8,128)S(1)}, f32[128,128]{1,0:T(8,128)S(1)}, u32[]{:S(2)}, u32[]{:S(2)}) collective-permute-start(f32[128,128]{1,0:T(8,128)S(1)} %get-tuple-element.40), channel_id=1, source_target_pairs={{0,8},{4,12},{8,0},{12,4},{1,9},{5,13},{9,1},{13,5},{2,10},{6,14},... | collective-permute-start | bytes 196616 | tf_op jit(solution)/shard_map/ppermute | solution.py:385
  28.8 6.1 %collective-permute-start.9 = (f32[128,128]{1,0:T(8,128)S(1)}, f32[128,128]{1,0:T(8,128)S(1)}, u32[]{:S(2)}, u32[]{:S(2)}) collective-permute-start(f32[128,128]{1,0:T(8,128)S(1)} %get-tuple-element.41), channel_id=1, source_target_pairs={{0,12},{4,8},{8,4},{12,0},{1,13},{5,9},{9,5},{13,1},{2,14},{6,10},... | collective-permute-start | bytes 196616 | tf_op jit(solution)/shard_map/ppermute | solution.py:385
  30.2 12.3 %collective-permute-start.6 = (f32[2,12,32,128]{3,2,1,0:T(8,128)S(1)}, f32[2,12,32,128]{3,2,1,0:T(8,128)S(1)}, u32[]{:S(2)}, u32[]{:S(2)}) collective-permute-start(f32[2,12,32,128]{3,2,1,0:T(8,128)S(1)} %get-tuple-element.38), channel_id=1, source_target_pairs={{0,2},{2,0},{1,3},{3,1},{4,6},{6,4},{5,7},{7,5},{8,10},{10,8},{9,1... | collective-permute-start | bytes 1179656 | tf_op jit(solution)/shard_map/ppermute | solution.py:393
  30.7 11.7 %collective-permute-start.10 = (f32[2,4,32,128]{3,2,1,0:T(8,128)S(1)}, f32[2,4,32,128]{3,2,1,0:T(8,128)S(1)}, u32[]{:S(2)}, u32[]{:S(2)}) collective-permute-start(f32[2,4,32,128]{3,2,1,0:T(8,128)S(1)} %get-tuple-element.44), channel_id=1, source_target_pairs={{0,2},{2,0},{1,3},{3,1},{4,6},{6,4},{5,7},{7,5},{8,10},{10,8},{9,1... | collective-permute-start | bytes 393224 | tf_op jit(solution)/shard_map/ppermute | solution.py:393
  35.5 7.1 %collective-permute-start.12 = (f32[8,16,128]{2,1,0:T(8,128)S(1)}, f32[8,16,128]{2,1,0:T(8,128)S(1)}, u32[]{:S(2)}, u32[]{:S(2)}) collective-permute-start(f32[8,16,128]{2,1,0:T(8,128)S(1)} %pad_maximum_fusion), channel_id=1, source_target_pairs={{0,1},{1,0},{2,3},{3,2},{4,5},{5,4},{6,7},{7,6},{8,9},{9,8},{10,11... | collective-permute-start | bytes 196616 | tf_op jit(solution)/shard_map/ppermute | solution.py:480
  42.4 6.8 %collective-permute-start.11 = (f32[2,4,32,128]{3,2,1,0:T(8,128)S(1)}, f32[2,4,32,128]{3,2,1,0:T(8,128)S(1)}, u32[]{:S(2)}, u32[]{:S(2)}) collective-permute-start(f32[2,4,32,128]{3,2,1,0:T(8,128)S(1)} %add.74), channel_id=1, source_target_pairs={{0,4},{2,14},{4,8},{6,2},{8,12},{10,6},{12,0},{14,10},{1,5},{3,15}... | collective-permute-start | bytes 393224 | tf_op jit(solution)/shard_map/ppermute | solution.py:459
  42.5 6.7 %collective-permute-start.13 = (f32[8,16,128]{2,1,0:T(8,128)S(1)}, f32[8,16,128]{2,1,0:T(8,128)S(1)}, u32[]{:S(2)}, u32[]{:S(2)}) collective-permute-start(f32[8,16,128]{2,1,0:T(8,128)S(1)} %pad_maximum_fusion.1), channel_id=1, source_target_pairs={{0,1},{1,0},{2,3},{3,2},{4,5},{5,4},{6,7},{7,6},{8,9},{9,8},{10,11... | collective-permute-start | bytes 196616 | tf_op jit(solution)/shard_map/ppermute | solution.py:480
